TPU v7x, 128 devices: a whole 4x4x4 slice. The times are simulated.
128 devices in a mesh: dp: 16 (over y_hi, x, core), row: 4 (over z), col: 2 (over y_lo).
Axes of the slice: x: 4, y: 4 (y_hi: 2, y_lo: 2; y = y_hi * 2 + y_lo), z: 4, core: 2. Of those that a mesh axis runs over, the one named last changes fastest.
Arguments:
- x_in: bfloat16 [8192, 1024], P('dp', 'row'), may hold values from -24 to 24
- segments: int32 [16, 512], P('dp'), may hold values from 0 to 3, never falling along the last dimension, each value on 1 to 256 neighbouring positions
- expert_ids: int32 [8192, 8], P('dp'), may hold values from 0 to 31, all different within a row; in each aligned block of 512 rows (0 to 511, 512 to 1023, ...) at most 160 rows name the same one
- cotangent: bfloat16 [8192, 1024], P('dp', 'row'), may hold values from -6 to 6
- norm_gain1: float32 [1024], P('row'), may hold values from 0.5 to 1.5
- w_query: bfloat16 [1024, 1024], P('row', 'col'), may hold values from -12 to 12
- w_key: bfloat16 [1024, 512], P('row', 'col'), may hold values from -1 to 1
- w_value: bfloat16 [1024, 512], P('row', 'col'), may hold values from -0.1875 to 0.1875
- w_out: bfloat16 [1024, 1024], P('col', 'row'), may hold values from -1.5 to 1.5
- norm_gain2: float32 [1024], P('row'), may hold values from 0.5 to 1.5
- w_router: bfloat16 [1024, 32], P('row'), may hold values from -24 to 24
- w_gate: bfloat16 [32, 1024, 512], P(None, 'row', 'col'), may hold values from -0.1875 to 0.1875
- w_up: bfloat16 [32, 1024, 512], P(None, 'row', 'col'), may hold values from -0.1875 to 0.1875
- w_down: bfloat16 [32, 512, 1024], P(None, 'col', 'row'), may hold values from -0.25 to 0.25
Outputs:
- block_out: bfloat16 [8192, 1024], P('dp', 'row')
- grad_input: bfloat16 [8192, 1024], P('dp', 'row')
- grad_query: float32 [1024, 1024], P('row', 'col')
- grad_key: float32 [1024, 512], P('row', 'col')
- grad_value: float32 [1024, 512], P('row', 'col')
- grad_out: float32 [1024, 1024], P('col', 'row')
- grad_router: float32 [1024, 32], P('row')
- grad_gate: float32 [32, 1024, 512], P('dp', 'row', 'col')
- grad_up: float32 [32, 1024, 512], P('dp', 'row', 'col')
- grad_down: float32 [32, 512, 1024], P('dp', 'col', 'row')
- grad_gain1: float32 [1024], P('row')
- grad_gain2: float32 [1024], P('row')
Inputs may be any that keep to these rules, and one draw needn't show every extreme that they name: `expert_ids`: each token names 8 different experts; within one sequence no expert is named by more than 160 tokens, and in some sequence one is named by exactly 160. `segments`: segment numbers never fall along a sequence; a segment holds at most 256 tokens, and some segment holds exactly that many.
All inputs are finite; a program needn't handle non-finite values.
Results may differ from a plain program's by a relative error of at most 0.0117.
The roundings to bfloat16 on the way count: a program that leaves them out, or rounds other values in their place, can miss the bound.
Values may be sent and summed in bfloat16 or wider, within the bound.
A program may use at most 192 MiB of HBM per device.

v0:
```python
import jax
import jax.numpy as jnp
from jax import lax
from jax.sharding import PartitionSpec as P

D = 1024
HEAD_DIM = 64
EXPERTS = 32
TOPK = 8
CAP = 160


EPSILON = 1e-06
ROPE_BASE = 10000.0
MASKED = -1e30


def rope_tables(positions):
    half_dim = HEAD_DIM // 2
    exponent = jnp.arange(half_dim).astype(jnp.float32) * (2.0 / HEAD_DIM)
    angles = positions.astype(jnp.float32)[:, None] * (ROPE_BASE ** (-exponent))[None, :]
    return (jnp.cos(angles)[:, None, :], jnp.sin(angles)[:, None, :])


def rotate(values_in, cosine, sine_part):
    half_dim = values_in.shape[-1] // 2
    low_half = values_in[..., :half_dim]
    high_half = values_in[..., half_dim:]
    return jnp.concatenate(
        [low_half * cosine - high_half * sine_part, high_half * cosine + low_half * sine_part],
        axis=-1,
    )


def slot_tables(route_rows):
    count_pairs = route_rows.shape[0] * route_rows.shape[1]
    flat_routes = route_rows.reshape(-1)
    expert_hits = (flat_routes[:, None] == jnp.arange(EXPERTS, dtype=jnp.int32)[None, :]).astype(
        jnp.int32
    )
    running = jnp.cumsum(expert_hits, axis=0)
    before = jnp.sum((running - 1) * expert_hits, axis=1)
    slot_of = flat_routes * CAP + before
    pair_of = (
        jnp.full((EXPERTS * CAP,), count_pairs, jnp.int32)
        .at[slot_of]
        .set(jnp.arange(count_pairs, dtype=jnp.int32))
    )
    return (slot_of, pair_of)


def row_total(vector):
    return lax.psum(vector, "row")


def col_total(matrix):
    return lax.psum(matrix, "col")


def head_share(matrix):
    return lax.psum_scatter(matrix, "row", scatter_dimension=0, tiled=True)


def head_collect(matrix):
    return lax.all_gather(matrix, "row", axis=0, tiled=True)


def slot_share(matrix):
    return lax.psum_scatter(matrix, "row", scatter_dimension=0, tiled=True)


def slot_collect(matrix):
    return lax.all_gather(matrix, "row", axis=0, tiled=True)


def norm_inverse(residual):
    squares = row_total(jnp.sum(residual * residual, axis=1))
    return lax.rsqrt(squares / D + EPSILON)[:, None]


def norm_backward(residual, inverse, gain, grad_normed):
    weighted = grad_normed * gain
    project = (row_total(jnp.sum(weighted * residual, axis=1)) / D)[:, None]
    grad_residual = inverse * weighted - residual * inverse**3 * project
    grad_gain = jnp.sum(grad_normed * residual * inverse, axis=0)
    return (grad_residual, grad_gain)


def on_device(
    x_in,
    segments,
    expert_ids,
    cotangent,
    norm_gain1,
    w_query,
    w_key,
    w_value,
    w_out,
    norm_gain2,
    w_router,
    w_gate,
    w_up,
    w_down,
):
    f32 = jnp.float32
    low = jnp.bfloat16
    length = x_in.shape[0]
    feature_part = x_in.shape[1]
    quarters = lax.axis_size("row")
    own_rows = length // quarters
    own_start = lax.axis_index("row") * own_rows
    query_width = w_query.shape[1]
    key_width = w_key.shape[1]
    heads_here = query_width // HEAD_DIM
    key_heads = key_width // HEAD_DIM
    group_size = heads_here // key_heads
    score_scale = HEAD_DIM ** (-0.5)
    residual = x_in.astype(f32)
    scale_attn = norm_inverse(residual)
    normed_attn = (residual * scale_attn * norm_gain1).astype(low)
    joined_proj = jnp.concatenate([w_query, w_key, w_value], axis=1)
    projected = head_share(jnp.dot(normed_attn, joined_proj, preferred_element_type=f32))
    positions = own_start + jnp.arange(own_rows, dtype=jnp.int32)
    cosine, sine_part = rope_tables(positions)
    queries = rotate(
        projected[:, :query_width].reshape(own_rows, heads_here, HEAD_DIM), cosine, sine_part
    ).astype(low)
    own_keys = rotate(
        projected[:, query_width : query_width + key_width].reshape(own_rows, key_heads, HEAD_DIM),
        cosine,
        sine_part,
    ).astype(low)
    own_values = projected[:, query_width + key_width :].astype(low)
    key_value = head_collect(
        jnp.concatenate([own_keys.reshape(own_rows, key_width), own_values], axis=1)
    )
    keys_wide = jnp.repeat(
        key_value[:, :key_width].reshape(length, key_heads, HEAD_DIM), group_size, axis=1
    )
    values_wide = jnp.repeat(
        key_value[:, key_width:].reshape(length, key_heads, HEAD_DIM), group_size, axis=1
    )
    segment_all = segments.reshape(-1)
    key_places = jnp.arange(length, dtype=jnp.int32)
    block_rows = min(256, own_rows)
    blocks = own_rows // block_rows
    query_blocks = queries.reshape(blocks, block_rows, heads_here, HEAD_DIM)
    place_blocks = positions.reshape(blocks, block_rows)
    segment_blocks = lax.dynamic_slice_in_dim(segment_all, own_start, own_rows).reshape(
        blocks, block_rows
    )

    def block_scores(query_block, place_block, segment_block):
        scores = (
            jnp.einsum("qhd,khd->hqk", query_block, keys_wide, preferred_element_type=f32)
            * score_scale
        )
        allowed = (key_places[None, :] <= place_block[:, None]) & (
            segment_all[None, :] == segment_block[:, None]
        )
        return jnp.where(allowed[None], scores, MASKED)

    def forward_block(unused_carry, inputs):
        query_block, place_block, segment_block = inputs
        scores = block_scores(query_block, place_block, segment_block)
        top_score = jnp.max(scores, axis=2, keepdims=True)
        log_total = top_score + jnp.log(jnp.sum(jnp.exp(scores - top_score), axis=2, keepdims=True))
        weights_low = jnp.exp(scores - log_total).astype(low)
        attended = jnp.einsum(
            "hqk,khd->qhd", weights_low, values_wide, preferred_element_type=f32
        ).astype(low)
        return (unused_carry, (attended, log_total))

    _, (attended_blocks, total_blocks) = lax.scan(
        forward_block, jnp.zeros((), jnp.int32), (query_blocks, place_blocks, segment_blocks)
    )
    attended_all = head_collect(attended_blocks.reshape(own_rows, query_width))
    resid_mid = residual + col_total(jnp.dot(attended_all, w_out, preferred_element_type=f32))
    scale_ffn = norm_inverse(resid_mid)
    normed_ffn = (resid_mid * scale_ffn * norm_gain2).astype(low)
    logits = lax.psum(jnp.dot(normed_ffn, w_router, preferred_element_type=f32), "row")
    gate_probs = jax.nn.softmax(jnp.take_along_axis(logits, expert_ids, axis=1), axis=1)
    slot_of, pair_of = slot_tables(expert_ids)
    owner_row = pair_of // TOPK
    padded = jnp.concatenate([normed_ffn, jnp.zeros((1, feature_part), low)], axis=0)
    dispatched = jnp.take(padded, owner_row, axis=0).reshape(EXPERTS, CAP, feature_part)
    both_weights = jnp.concatenate([w_gate, w_up], axis=2)
    hidden_width = w_gate.shape[2]
    pre_act = jnp.einsum("ecd,edf->ecf", dispatched, both_weights, preferred_element_type=f32)
    pre_own = slot_share(pre_act.reshape(EXPERTS * CAP, 2 * hidden_width))
    gate_act = pre_own[:, :hidden_width]
    up_act = pre_own[:, hidden_width:]
    sigmoid_gate = jax.nn.sigmoid(gate_act)
    hidden_own = (gate_act * sigmoid_gate * up_act).astype(low)
    hidden_all = slot_collect(hidden_own).reshape(EXPERTS, CAP, hidden_width)
    expert_out = jnp.einsum("ecf,efd->ecd", hidden_all, w_down, preferred_element_type=f32).reshape(
        EXPERTS * CAP, feature_part
    )
    picked = jnp.take(expert_out, slot_of, axis=0).reshape(length, TOPK, feature_part)
    resid_out = resid_mid + col_total(jnp.sum(gate_probs[:, :, None] * picked, axis=1))
    block_out = resid_out.astype(low)
    grad_top = cotangent.astype(f32)
    grad_prob = lax.psum(jnp.sum(grad_top[:, None, :] * picked, axis=2), ("row", "col"))
    grad_chosen = gate_probs * (grad_prob - jnp.sum(gate_probs * grad_prob, axis=1, keepdims=True))
    expert_hits = (
        expert_ids[:, :, None] == jnp.arange(EXPERTS, dtype=jnp.int32)[None, None, :]
    ).astype(f32)
    grad_logits = jnp.sum(expert_hits * grad_chosen[:, :, None], axis=1).astype(low)
    grad_router = jnp.dot(normed_ffn.T, grad_logits, preferred_element_type=f32)
    spread = (gate_probs[:, :, None] * grad_top[:, None, :]).reshape(length * TOPK, feature_part)
    spread = jnp.concatenate([spread, jnp.zeros((1, feature_part), f32)], axis=0)
    slot_grad = jnp.take(spread, pair_of, axis=0).astype(low).reshape(EXPERTS, CAP, feature_part)
    hidden_grad = slot_share(
        jnp.einsum("ecd,efd->ecf", slot_grad, w_down, preferred_element_type=f32).reshape(
            EXPERTS * CAP, hidden_width
        )
    )
    grad_pre = jnp.concatenate(
        [
            hidden_grad * up_act * sigmoid_gate * (1.0 + gate_act * (1.0 - sigmoid_gate)),
            hidden_grad * gate_act * sigmoid_gate,
        ],
        axis=1,
    ).astype(low)
    grad_pre_all = slot_collect(grad_pre).reshape(EXPERTS, CAP, 2 * hidden_width)
    slot_input = jnp.einsum(
        "ecf,edf->ecd", grad_pre_all, both_weights, preferred_element_type=f32
    ).reshape(EXPERTS * CAP, feature_part)
    grad_both_full = jnp.einsum(
        "ecd,ecf->edf", dispatched, grad_pre_all, preferred_element_type=f32
    )
    grad_down_full = jnp.einsum("ecf,ecd->efd", hidden_all, slot_grad, preferred_element_type=f32)
    grad_both, grad_down = (
        lax.psum_scatter(grad_both_full, "dp", scatter_dimension=0, tiled=True),
        lax.psum_scatter(grad_down_full, "dp", scatter_dimension=0, tiled=True),
    )
    grad_gate = grad_both[:, :, :hidden_width]
    grad_up = grad_both[:, :, hidden_width:]
    token_grad = jnp.sum(
        jnp.take(slot_input, slot_of, axis=0).reshape(length, TOPK, feature_part), axis=1
    )
    grad_normed_ffn = col_total(token_grad) + jnp.dot(
        grad_logits, w_router.T, preferred_element_type=f32
    )
    grad_ffn_in, grad_gain2 = norm_backward(resid_mid, scale_ffn, norm_gain2, grad_normed_ffn)
    grad_mid = grad_top + grad_ffn_in
    grad_mid_low = grad_mid.astype(low)
    grad_out_part = jnp.dot(attended_all.T, grad_mid_low, preferred_element_type=f32)
    grad_attended = head_share(jnp.dot(grad_mid_low, w_out.T, preferred_element_type=f32)).astype(
        low
    )
    grad_blocks = grad_attended.reshape(blocks, block_rows, heads_here, HEAD_DIM)

    def backward_block(carry, inputs):
        key_acc, value_acc = carry
        query_block, place_block, segment_block, attended_block, total_block, grad_block = inputs
        scores = block_scores(query_block, place_block, segment_block)
        weights = jnp.exp(scores - total_block)
        value_step = jnp.einsum(
            "hqk,qhd->khd", weights.astype(low), grad_block, preferred_element_type=f32
        )
        grad_weights = jnp.einsum(
            "qhd,khd->hqk", grad_block, values_wide, preferred_element_type=f32
        )
        delta_sum = jnp.sum(grad_block.astype(f32) * attended_block.astype(f32), axis=2).T[
            :, :, None
        ]
        grad_scores = (weights * (grad_weights - delta_sum)).astype(low)
        grad_query_block = (
            jnp.einsum("hqk,khd->qhd", grad_scores, keys_wide, preferred_element_type=f32)
            * score_scale
        )
        key_step = (
            jnp.einsum("hqk,qhd->khd", grad_scores, query_block, preferred_element_type=f32)
            * score_scale
        )
        return ((key_acc + key_step, value_acc + value_step), grad_query_block)

    zeros_wide = jnp.zeros((length, heads_here, HEAD_DIM), f32)
    (key_acc, value_acc), grad_query_blocks = lax.scan(
        backward_block,
        (zeros_wide, zeros_wide),
        (query_blocks, place_blocks, segment_blocks, attended_blocks, total_blocks, grad_blocks),
    )
    key_partial = jnp.sum(key_acc.reshape(length, key_heads, group_size, HEAD_DIM), axis=2).reshape(
        length, key_width
    )
    value_partial = jnp.sum(
        value_acc.reshape(length, key_heads, group_size, HEAD_DIM), axis=2
    ).reshape(length, key_width)
    key_value_grad = head_share(jnp.concatenate([key_partial, value_partial], axis=1))
    grad_queries = (
        rotate(grad_query_blocks.reshape(own_rows, heads_here, HEAD_DIM), cosine, -sine_part)
        .astype(low)
        .reshape(own_rows, query_width)
    )
    grad_keys = (
        rotate(
            key_value_grad[:, :key_width].reshape(own_rows, key_heads, HEAD_DIM), cosine, -sine_part
        )
        .astype(low)
        .reshape(own_rows, key_width)
    )
    grad_values = key_value_grad[:, key_width:].astype(low)
    grad_proj = head_collect(jnp.concatenate([grad_queries, grad_keys, grad_values], axis=1))
    grad_joined = jnp.dot(normed_attn.T, grad_proj, preferred_element_type=f32)
    grad_normed_attn = col_total(jnp.dot(grad_proj, joined_proj.T, preferred_element_type=f32))
    grad_attn_in, grad_gain1 = norm_backward(residual, scale_attn, norm_gain1, grad_normed_attn)
    grad_input = (grad_mid + grad_attn_in).astype(low)
    joined_sum, out_sum, router_sum, gain1_sum, gain2_sum = lax.psum(
        (grad_joined, grad_out_part, grad_router, grad_gain1, grad_gain2), "dp"
    )
    return (
        block_out,
        grad_input,
        joined_sum[:, :query_width],
        joined_sum[:, query_width : query_width + key_width],
        joined_sum[:, query_width + key_width :],
        out_sum,
        router_sum,
        grad_gate,
        grad_up,
        grad_down,
        gain1_sum,
        gain2_sum,
    )


def solution(mesh):
    placed = (
        P("dp", "row"),
        P("dp", None),
        P("dp", None),
        P("dp", "row"),
        P("row"),
        P("row", "col"),
        P("row", "col"),
        P("row", "col"),
        P("col", "row"),
        P("row"),
        P("row", None),
        P(None, "row", "col"),
        P(None, "row", "col"),
        P(None, "col", "row"),
    )
    return jax.shard_map(
        on_device,
        mesh=mesh,
        in_specs=placed,
        out_specs=(
            P("dp", "row"),
            P("dp", "row"),
            P("row", "col"),
            P("row", "col"),
            P("row", "col"),
            P("col", "row"),
            P("row", None),
            P("dp", "row", "col"),
            P("dp", "row", "col"),
            P("dp", "col", "row"),
            P("row"),
            P("row"),
        ),
        check_vma=False,
    )
```

profile of v0, /device:TPU:1, one launch (start us, length us, event | category | flops | bytes accessed | tf_op | source)
XLA Modules:
  0.0 1183.6 jit_solution(17169282977297748467)
XLA Ops:
  8.4 10.6 psum.105
  26.8 9.2 reduce-window.6
  37.7 15.5 %scatter_custom_fusion = s32[5120]{0:T(1024)S(1)} fusion(s32[4096]{0:T(1024)S(1)} %bitcast.134, s32[4096]{0:T(1024)S(1)} %iota.35, s32[]{:T(128)} %constant.152.clone.1), kind=kCustom, calls=%fused_computation.130 | custom fusion | bytes 20484 | tf_op jit(solution)/shard_map/scatter | solution.py:47
  60.6 9.9 all_gather.15
  73.9 11.3 all_gather.16
  96.7 31.8 %all-reduce.11.cloned.1.call-done = f32[512,256]{1,0:T(8,128)} async-done(((f32[512,256]{1,0:T(8,128)}), f32[512,256]{1,0:T(8,128)}) %all-reduce.11.cloned.1.call-update) | async-done | bytes 524304 | tf_op jit(solution)/shard_map/psum | solution.py:57
  129.7 8.7 psum.107
  139.2 18.2 %gather_fusion = bf16[5120,256]{1,0:T(8,128)(2,1)S(1)} fusion(bf16[513,256]{1,0:T(8,128)(2,1)S(1)} %concatenate.45, s32[5120]{0:T(1024)S(1)} %get-tuple-element.121), kind=kCustom, calls=%fused_computation.2 | custom fusion | bytes 5263360 | tf_op jit(solution)/shard_map/jit(_take)/gather | solution.py:186
  157.4 8.1 fusion.3
  167.1 97.0 %reduce-scatter.10.cloned.1.call-done = f32[1280,512]{1,0:T(8,128)} async-done(((f32[5120,512]{1,0:T(8,128)}), f32[1280,512]{1,0:T(8,128)}) %reduce-scatter.10.cloned.1.call-update) | async-done | bytes 2621456 | tf_op jit(solution)/shard_map/reduce_scatter | solution.py:69
  267.8 37.8 %all-reduce.13.cloned.1.call-done = f32[512,32]{0,1:T(8,128)} async-done(((f32[512,32]{0,1:T(8,128)}), f32[512,32]{0,1:T(8,128)}) %all-reduce.13.cloned.1.call-update) | async-done | bytes 65552 | tf_op jit(solution)/shard_map/psum | solution.py:181
  305.5 28.9 %gather_fusion.2 = f32[4096]{0:T(1024)S(1)} fusion(f32[512,32]{0,1:T(8,128)} %all-reduce.13.cloned.1.call-done, s32[4096]{0:T(1024)S(1)} %reshape.440), kind=kCustom, calls=%fused_computation.4 | custom fusion | bytes 65536 | tf_op jit(solution)/shard_map/jit(take_along_axis)/gather | solution.py:182
  334.8 10.1 all-gather.4.cloned.1.call-done
  351.0 18.7 %gather_fusion.3 = f32[4096,256]{1,0:T(8,128)} fusion(f32[5120,256]{1,0:T(8,128)} %bitcast.103, s32[4096]{0:T(1024)S(1)} %broadcast_clamp_fusion.1), kind=kCustom, calls=%fused_computation.clone | custom fusion | bytes 8404992 | tf_op jit(solution)/shard_map/jit(_take)/gather | solution.py:199
  372.8 25.3 %psum.111 = f32[512,8]{0,1:T(8,128)S(1)} all-reduce(f32[512,8]{0,1:T(8,128)S(1)} %copy.81), channel_id=1, replica_groups=mesh['dp'=16,'row'=4,'col'=2] {'row','col'}, use_global_device_ids=true, to_apply=%region_22.24 | all-reduce | flops 4096 | bytes 32768 | tf_op jit(solution)/shard_map/psum | solution.py:203
  400.4 21.0 %gather_fusion.1 = bf16[5120,256]{1,0:T(8,128)(2,1)} fusion(bf16[4097,256]{1,0:T(8,128)(2,1)S(1)} %concatenate.47, s32[5120]{0:T(1024)S(1)} %get-tuple-element.120), kind=kCustom, calls=%fused_computation.3 | custom fusion | bytes 5263360 | tf_op jit(solution)/shard_map/jit(_take)/gather | solution.py:212
  428.4 61.2 %reduce-scatter.12.cloned.1.call-done = f32[1280,256]{1,0:T(8,128)} async-done(((f32[5120,256]{1,0:T(8,128)}), f32[1280,256]{1,0:T(8,128)}) %reduce-scatter.12.cloned.1.call-update) | async-done | bytes 1310736 | tf_op jit(solution)/shard_map/reduce_scatter | solution.py:69
  492.8 56.8 %all-gather.6.cloned.1.call-done = bf16[5120,512]{1,0:T(8,128)(2,1)} async-done(((bf16[1280,512]{1,0:T(8,128)(2,1)}), bf16[5120,512]{1,0:T(8,128)(2,1)}) %all-gather.6.cloned.1.call-update) | async-done | bytes 5242896 | tf_op jit(solution)/shard_map/all_gather | solution.py:73
  549.6 10.1 fusion.64
  559.7 18.7 %gather_fusion.4 = f32[4096,256]{1,0:T(8,128)} fusion(f32[5120,256]{1,0:T(8,128)} %bitcast.102, s32[4096]{0:T(1024)S(1)} %broadcast_clamp_fusion.1), kind=kCustom, calls=%fused_computation.1.clone | custom fusion | bytes 8404992 | tf_op jit(solution)/shard_map/jit(_take)/gather | solution.py:240
  586.4 35.6 %all-reduce.15.cloned.1.call-done = f32[512,256]{1,0:T(8,128)} async-done(((f32[512,256]{1,0:T(8,128)}), f32[512,256]{1,0:T(8,128)}) %all-reduce.15.cloned.1.call-update) | async-done | bytes 524304 | tf_op jit(solution)/shard_map/psum | solution.py:57
  624.7 8.6 psum.112
  636.5 22.2 %reduce-scatter.14.cloned.1.call-done = f32[128,512]{1,0:T(8,128)} async-done(((f32[512,512]{1,0:T(8,128)}), f32[128,512]{1,0:T(8,128)}) %reduce-scatter.14.cloned.1.call-update) | async-done | bytes 262160 | tf_op jit(solution)/shard_map/reduce_scatter | solution.py:61
  667.9 22.7 %reduce-scatter.16.cloned.1.call-done = f32[128,512]{0,1:T(8,128)} async-done(((f32[512,512]{0,1:T(8,128)}), f32[128,512]{0,1:T(8,128)}) %reduce-scatter.16.cloned.1.call-update) | async-done | bytes 262160 | tf_op jit(solution)/shard_map/reduce_scatter | solution.py:61
  693.3 26.6 %all-gather.8.cloned.1.call-done = bf16[512,1024]{0,1:T(8,128)(2,1)} async-done(((bf16[128,1024]{0,1:T(8,128)(2,1)}), bf16[512,1024]{0,1:T(8,128)(2,1)}) %all-gather.8.cloned.1.call-update) | async-done | bytes 1048592 | tf_op jit(solution)/shard_map/all_gather | solution.py:65
  727.9 9.3 fusion.2
  745.8 26.2 %all-reduce.19.cloned.1.call-done = (f32[512,256]{1,0:T(8,128)}, f32[512,256]{1,0:T(8,128)}) async-done(((f32[512,256]{1,0:T(8,128)}, f32[512,256]{1,0:T(8,128)}), (f32[512,256]{1,0:T(8,128)}, f32[512,256]{1,0:T(8,128)})) %all-reduce.19.cloned.1.call-update) | async-done | bytes 1048592 | tf_op jit(solution)/shard_map/psum | solution.py:57
  773.3 8.7 psum.114
  781.9 64.4 %all-reduce.2 = (f32[256,32]{0,1:T(8,128)}, f32[256]{0:T(256)}, f32[256]{0:T(256)}) all-reduce(f32[256,32]{0,1:T(8,128)S(1)} %fusion.66, f32[256]{0:T(256)S(1)} %get-tuple-element.73, f32[256]{0:T(256)S(1)} %copy-done.50), channel_id=1, replica_groups=mesh['dp'=16,'row'=4,'col'=2] {'dp'}, use_global_device_ids=true, to_apply=%region_37.39 | all-reduce | flops 8704 | bytes 69632 | tf_op jit(solution)/shard_map/psum | solution.py:310
  850.1 68.4 %all-reduce.17.cloned.1.call-done = (f32[256,1024]{1,0:T(8,128)}, f32[512,256]{1,0:T(8,128)}) async-done(((f32[256,1024]{1,0:T(8,128)}, f32[512,256]{1,0:T(8,128)}), (f32[256,1024]{1,0:T(8,128)}, f32[512,256]{1,0:T(8,128)})) %all-reduce.17.cloned.1.call-update) | async-done | bytes 1572880 | tf_op jit(solution)/shard_map/psum | solution.py:310
  922.3 149.0 %reduce-scatter.18.cloned.1.call-done = f32[2,256,512]{2,1,0:T(8,128)} async-done(((f32[32,256,512]{2,1,0:T(8,128)}), f32[2,256,512]{2,1,0:T(8,128)}) %reduce-scatter.18.cloned.1.call-update) | async-done | bytes 1048592 | tf_op jit(solution)/shard_map/reduce_scatter | solution.py:234
  1073.5 102.7 %reduce-scatter.20.cloned.1.call-done = f32[2,256,256]{2,1,0:T(8,128)} async-done(((f32[32,256,256]{2,1,0:T(8,128)}), f32[2,256,256]{2,1,0:T(8,128)}) %reduce-scatter.20.cloned.1.call-update) | async-done | bytes 524304 | tf_op jit(solution)/shard_map/reduce_scatter | solution.py:235
  (248 shorter events, 115.5 us)
Async XLA Ops:
  7.2 78.8 %copy-start = (bf16[512,256]{1,0:T(8,128)(2,1)S(1)}, bf16[512,256]{1,0:T(8,128)(2,1)}, u32[]{:S(2)}) copy-start(bf16[512,256]{1,0:T(8,128)(2,1)} %param.24) | copy-start | bytes 786436
  7.2 50.1 %reduce-scatter.8.cloned.1.call-start = ((), (), s32[]{:S(2)}) async-start(), calls=%async_computation.7 | async-start | bytes 2621440 | tf_op jit(solution)/shard_map/reduce_scatter | solution.py:61
  26.0 102.6 %all-reduce.11.cloned.1.call-start = ((), (), s32[]{:S(2)}) async-start(), calls=%async_computation.8 | async-start | bytes 1048576 | tf_op jit(solution)/shard_map/psum | solution.py:57
  87.2 176.9 %reduce-scatter.10.cloned.1.call-start = ((), (), s32[]{:S(2)}) async-start(), calls=%async_computation.10 | async-start | bytes 13107200 | tf_op jit(solution)/shard_map/reduce_scatter | solution.py:69
  92.0 36.5 %copy-start.9 = (bf16[512,256]{1,0:T(8,128)(2,1)S(1)}, bf16[512,256]{1,0:T(8,128)(2,1)}, u32[]{:S(2)}) copy-start(bf16[512,256]{1,0:T(8,128)(2,1)} %param.16) | copy-start | bytes 786436
  92.0 47.0 %copy-start.45 = (f32[256]{0:T(256)S(1)}, f32[256]{0:T(256)}, u32[]{:S(2)}) copy-start(f32[256]{0:T(256)} %param.25) | copy-start | bytes 3076
  165.5 102.2 %copy-start.27 = (bf16[512,256]{1,0:T(8,128)(2,1)S(1)}, bf16[512,256]{1,0:T(8,128)(2,1)}, u32[]{:S(2)}) copy-start(bf16[512,256]{1,0:T(8,128)(2,1)} %param.19) | copy-start | bytes 786436
  165.5 140.0 %all-reduce.13.cloned.1.call-start = ((), (), s32[]{:S(2)}) async-start(), calls=%async_computation.9 | async-start | bytes 131072 | tf_op jit(solution)/shard_map/psum | solution.py:181
  167.0 177.8 %all-gather.4.cloned.1.call-start = ((), (), s32[]{:S(2)}) async-start(), calls=%async_computation.11 | async-start | bytes 3276800 | tf_op jit(solution)/shard_map/all_gather | solution.py:73
  267.1 222.5 %reduce-scatter.12.cloned.1.call-start = ((), (), s32[]{:S(2)}) async-start(), calls=%async_computation.12 | async-start | bytes 6553600 | tf_op jit(solution)/shard_map/reduce_scatter | solution.py:69
  428.3 61.3 %copy-start.8 = (f32[1280,512]{1,0:T(8,128)S(1)}, f32[1280,512]{1,0:T(8,128)}, u32[]{:S(2)}) copy-start(f32[1280,512]{1,0:T(8,128)} %reduce-scatter.10.cloned.1.call-done) | copy-start | bytes 7864324
  428.4 121.2 %all-gather.6.cloned.1.call-start = ((), (), s32[]{:S(2)}) async-start(), calls=%async_computation.13 | async-start | bytes 6553600 | tf_op jit(solution)/shard_map/all_gather | solution.py:73
  492.7 129.3 %all-reduce.15.cloned.1.call-start = ((), (), s32[]{:S(2)}) async-start(), calls=%async_computation.14 | async-start | bytes 1048576 | tf_op jit(solution)/shard_map/psum | solution.py:57
  578.4 43.6 %copy-start.7 = (f32[512,256]{1,0:T(8,128)S(1)}, f32[512,256]{1,0:T(8,128)}, u32[]{:S(2)}) copy-start(f32[512,256]{1,0:T(8,128)} %copy-done.6) | copy-start | bytes 1572868
  578.4 43.6 %copy-start.46 = (f32[256]{0:T(256)S(1)}, f32[256]{0:T(256)}, u32[]{:S(2)}) copy-start(f32[256]{0:T(256)} %param.25) | copy-start | bytes 3076
  578.4 54.9 %copy-start.49 = (f32[512]{0:T(512)S(1)}, f32[512]{0:T(512)}, u32[]{:S(2)}) copy-start(f32[512]{0:T(512)} %get-tuple-element.124) | copy-start | bytes 6148
  586.3 72.5 %reduce-scatter.14.cloned.1.call-start = ((), (), s32[]{:S(2)}) async-start(), calls=%async_computation.15 | async-start | bytes 1310720 | tf_op jit(solution)/shard_map/reduce_scatter | solution.py:61
  586.4 46.9 %copy-start.36 = (bf16[512,32]{0,1:T(8,128)(2,1)}, bf16[512,32]{0,1:T(8,128)(2,1)S(1)}, u32[]{:S(2)}) copy-start(bf16[512,32]{0,1:T(8,128)(2,1)S(1)} %select_reduce_fusion) | copy-start | bytes 98308
  633.3 29.1 %copy-start.2 = (f32[8,128,512]{2,1,0:T(8,128)S(1)}, f32[8,128,512]{2,1,0:T(8,128)}, u32[]{:S(2)}) copy-start(f32[8,128,512]{2,1,0:T(8,128)} %copy-done.1) | copy-start | bytes 6291460
  636.2 54.4 %reduce-scatter.16.cloned.1.call-start = ((), (), s32[]{:S(2)}) async-start(), calls=%async_computation.16 | async-start | bytes 1310720 | tf_op jit(solution)/shard_map/reduce_scatter | solution.py:61
  666.8 53.1 %copy-start.23 = (bf16[256,1024]{1,0:T(8,128)(2,1)S(1)}, bf16[256,1024]{1,0:T(8,128)(2,1)}, u32[]{:S(2)}) copy-start(bf16[256,1024]{1,0:T(8,128)(2,1)} %copy-done.22) | copy-start | bytes 1572868
  666.8 53.0 %all-gather.8.cloned.1.call-start = ((), (), s32[]{:S(2)}) async-start(), calls=%async_computation.17 | async-start | bytes 1310720 | tf_op jit(solution)/shard_map/all_gather | solution.py:65
  693.2 31.7 %copy-start.43 = (f32[512]{0:T(512)S(1)}, f32[512]{0:T(512)}, u32[]{:S(2)}) copy-start(f32[512]{0:T(512)} %copy-done.42) | copy-start | bytes 6148
  693.2 31.7 %copy-start.44 = (f32[256]{0:T(256)S(1)}, f32[256]{0:T(256)}, u32[]{:S(2)}) copy-start(f32[256]{0:T(256)} %param.20) | copy-start | bytes 3076
  693.2 78.7 %all-reduce.19.cloned.1.call-start = ((), (), s32[]{:S(2)}) async-start(), calls=%async_computation.21 | async-start | bytes 2097152 | tf_op jit(solution)/shard_map/psum | solution.py:57
  722.4 196.1 %all-reduce.17.cloned.1.call-start = ((), (), s32[]{:S(2)}) async-start(), calls=%async_computation.20 | async-start | bytes 3145728 | tf_op jit(solution)/shard_map/psum | solution.py:310
  727.9 343.4 %reduce-scatter.18.cloned.1.call-start = ((), (), s32[]{:S(2)}) async-start(), calls=%async_computation.18 | async-start | bytes 17825792 | tf_op jit(solution)/shard_map/reduce_scatter | solution.py:234
  737.2 439.0 %reduce-scatter.20.cloned.1.call-start = ((), (), s32[]{:S(2)}) async-start(), calls=%async_computation.19 | async-start | bytes 8912896 | tf_op jit(solution)/shard_map/reduce_scatter | solution.py:235
  744.7 37.2 %copy-start.50 = (f32[256]{0:T(256)S(1)}, f32[256]{0:T(256)}, u32[]{:S(2)}) copy-start(f32[256]{0:T(256)} %get-tuple-element.71) | copy-start | bytes 3076
  744.7 103.4 %copy-start.47 = (f32[512]{0:T(512)S(1)}, f32[512]{0:T(512)}, u32[]{:S(2)}) copy-start(f32[512]{0:T(512)} %get-tuple-element.122) | copy-start | bytes 6148
  745.6 102.4 %copy-start.14 = (f32[512,256]{1,0:T(8,128)S(1)}, f32[512,256]{1,0:T(8,128)}, u32[]{:S(2)}) copy-start(f32[512,256]{1,0:T(8,128)} %copy-done.13) | copy-start | bytes 1572868
  918.5 257.8 %copy-start.33 = (f32[512,256]{1,0:T(8,128)S(1)}, f32[512,256]{1,0:T(8,128)}, u32[]{:S(2)}) copy-start(f32[512,256]{1,0:T(8,128)} %get-tuple-element.139) | copy-start | bytes 1572868
  (35 other events, 253.1 us)
Sparse Core Ops, SparseCore 0:
  26.1 31.2 reduce-scatter.7
  87.3 41.1 all-reduce.10
  165.6 98.4 reduce-scatter.9
  266.9 38.6 all-reduce.12
  307.2 37.6 all-gather.3
  428.5 61.0 reduce-scatter.11
  492.9 56.6 all-gather.5
  586.4 35.5 all-reduce.14
  636.4 22.3 reduce-scatter.13
  667.0 23.5 reduce-scatter.15
  693.3 26.4 all-gather.7
  723.4 48.5 all-reduce.18
  775.3 143.2 all-reduce.16
  922.7 148.4 reduce-scatter.17
  1076.6 99.5 reduce-scatter.19
where the time goes:
time: 1190 us; the launch traced here: 1180 us
  waiting for transfers between devices  751 us (63%)
  local copies, waits for them, and re-layouts  157 us (13%)
  blocking collectives  147 us (12%)
  matrix products  66.9 us (6%)
  other arithmetic  44.7 us (4%)
  between operations  14.9 us (1%)
    reduce_scatter x2, waiting for transfers between devices, slot_share(): return lax.psum_scatter(matrix, 'row', scatter_dimension=0, tiled=True)  158 us
    reduce_scatter x1, waiting for transfers between devices, on_device(): lax.psum_scatter(grad_both_full, 'dp', scatter_dimension=0, tiled=True)  149 us
    reduce_scatter x1, waiting for transfers between devices, on_device(): lax.psum_scatter(grad_down_full, 'dp', scatter_dimension=0, tiled=True)  103 us
    psum x3, waiting for transfers between devices, col_total(): return lax.psum(matrix, 'col')  93.5 us
    psum x1, waiting for transfers between devices, on_device(): lax.psum((grad_joined, grad_out_part, grad_router, grad_gain1, grad_gain2...  68.4 us
    all_gather x2, waiting for transfers between devices, slot_collect(): return lax.all_gather(matrix, 'row', axis=0, tiled=True)  66.9 us
    psum x1, blocking collectives, on_device(): lax.psum((grad_joined, grad_out_part, grad_router, grad_gain1, grad_gain2...  64.4 us
    reduce_scatter x3, waiting for transfers between devices, head_share(): return lax.psum_scatter(matrix, 'row', scatter_dimension=0, tiled=True)  48.1 us
  transfers between devices with their start and end apart: 15, of which 15 were waited for; matrix products, arithmetic and copies ran while one was open for 9% of the time, Pallas kernels for 0%

commit v1 on v0

v1 whole, which is shorter than its diff:
```python
import jax
import jax.numpy as jnp
from jax import lax
from jax.experimental import pallas as pl
from jax.experimental.pallas import tpu as pltpu
from jax.sharding import PartitionSpec as P

D = 1024
HEAD_DIM = 64
EXPERTS = 32
CAP = 160
LENGTH = 512

EPSILON = 1e-06
ROPE_BASE = 10000.0
MASKED = -1e30
F32 = jnp.float32
LOW = jnp.bfloat16
MESH = pl.DeviceIdType.MESH

AXES = ("dp", "row", "col")
CORE = ("dp", 1, 2)
X = ("dp", 2, 4)
Y_HI = ("dp", 8, 2)
Z = ("row", 1, 4)
SIDE = ("col", 1, 2)
TEAM = (Z, SIDE)
PLANE = (Z, X)
ALL_DP = (CORE, X, Y_HI)


def size_of(group):
    n = 1
    for _, _, size in group:
        n *= size
    return n


def at(direction):
    axis, weight, size = direction
    return (lax.axis_index(axis) // weight) % size


def member(group):
    index, scale = 0, 1
    for direction in group:
        index = index + at(direction) * scale
        scale *= direction[2]
    return index


def steps_of(group):
    moves = [()]
    for direction in group:
        moves = [m + (k,) for m in moves for k in range(direction[2])]

    def way(move):
        return sum(
            min(k, d[2] - k) * (2 if d == Y_HI else 1) for d, k in zip(group, move)
        )

    return sorted([m for m in moves if any(m)], key=lambda m: -way(m))


def goal(group, move):
    index, scale = 0, 1
    place = {a: lax.axis_index(a) for a in AXES}
    for direction, k in zip(group, move):
        axis, weight, size = direction
        here = at(direction)
        there = (here + k) % size
        place[axis] = place[axis] + weight * (there - here)
        index = index + there * scale
        scale *= size
    return index, place


def expert_of(x, z, c):
    return c * 16 + x * 4 + z


def exchange(number, *items):
    modes = [i[0] for i in items]
    groups = [i[1] for i in items]
    arrays = [i[2] for i in items]
    count = len(items)
    most = max([8] + [size_of(g) for g in groups])
    moves = {}
    for g in groups:
        for move in steps_of(g):
            full = {d: k for d, k in zip(g, move) if k}
            moves[tuple(sorted(full.items()))] = (g, move)
    delivers = "deliver" in modes

    def kernel(*refs):
        ins, outs = refs[:count], refs[count : 2 * count]
        send, recv, local = refs[2 * count :]
        dp, z, c = (lax.axis_index(a) for a in AXES)
        y_hi, x, core = dp // 8, (dp // 2) % 4, dp % 2
        barrier = pltpu.get_barrier_semaphore()
        owner = c * 8 + x * 2 + z // 2
        slot = (z % 2) * 4 + y_hi * 2 + core
        for g, move in moves.values():
            pl.semaphore_signal(
                barrier, inc=1, device_id=goal(g, move)[1], device_id_type=MESH
            )
        sources = []
        if delivers:
            for i in range(8):
                place = {
                    "dp": ((i // 2) % 2) * 8 + x * 2 + i % 2,
                    "row": core * 2 + i // 4,
                    "col": y_hi,
                }
                mine = (place["dp"] == dp) & (place["row"] == z) & (place["col"] == c)
                sources.append((place, mine))

                @pl.when(jnp.logical_not(mine))
                def _(place=place):
                    pl.semaphore_signal(
                        barrier, inc=1, device_id=place, device_id_type=MESH
                    )

            @pl.when(owner == dp)
            def _():
                pl.semaphore_wait(barrier, len(moves) + 7)

            @pl.when(owner != dp)
            def _():
                pl.semaphore_wait(barrier, len(moves) + 8)

        else:
            pl.semaphore_wait(barrier, len(moves))

        def block(a, index, place):
            if modes[a] == "split":
                return ins[a].at[index]
            if modes[a] == "expert":
                e = expert_of(x, place["row"], place["col"])
                return ins[a].at[e, pl.ds(pl.multiple_of(core * 128, 128), 128), :]
            return ins[a]

        copies = []
        for a in range(count):
            if modes[a] == "deliver":
                continue
            me = member(groups[a])
            for step, move in enumerate(steps_of(groups[a])):
                index, place = goal(groups[a], move)
                copies.append(
                    pltpu.make_async_remote_copy(
                        src_ref=block(a, index, place),
                        dst_ref=outs[a] if modes[a] == "swap" else outs[a].at[me],
                        send_sem=send.at[a, step],
                        recv_sem=recv.at[a, step],
                        device_id=place,
                        device_id_type=MESH,
                    )
                )
                copies[-1].start()
        for a in range(count):
            if modes[a] not in ("swap", "deliver"):
                me = member(groups[a])
                source = block(a, me, {"row": z, "col": c})
                copies.append(pltpu.make_async_copy(source, outs[a].at[me], local.at[a]))
                copies[-1].start()
        for a in range(count):
            if modes[a] == "deliver":

                def remote(j, a=a):
                    return pltpu.make_async_remote_copy(
                        src_ref=ins[a].at[j],
                        dst_ref=outs[a].at[slot],
                        send_sem=send.at[a, j],
                        recv_sem=recv.at[a, slot],
                        device_id={"dp": owner, "row": j % 4, "col": j // 4},
                        device_id_type=MESH,
                    )

                def own(j):
                    return (owner == dp) & (z == j % 4) & (c == j // 4)

                for kz, kc in ((2, 1), (2, 0), (1, 1), (3, 1), (1, 0), (3, 0), (0, 1), (0, 0)):
                    j = (z + kz) % 4 + 4 * ((c + kc) % 2)

                    @pl.when(own(j))
                    def _(j=j, a=a):
                        copy = pltpu.make_async_copy(
                            ins[a].at[j], outs[a].at[slot], local.at[a]
                        )
                        copy.start()
                        copy.wait()

                    @pl.when(jnp.logical_not(own(j)))
                    def _(j=j):
                        remote(j).start()

                for j in range(8):

                    @pl.when(jnp.logical_not(own(j)))
                    def _(j=j):
                        remote(j).wait_send()

                for i in range(8):

                    @pl.when(jnp.logical_not(sources[i][1]))
                    def _(i=i, a=a):
                        pltpu.make_async_remote_copy(
                            src_ref=ins[a].at[0],
                            dst_ref=outs[a].at[i],
                            send_sem=send.at[a, 0],
                            recv_sem=recv.at[a, i],
                            device_id={"dp": owner, "row": 0, "col": 0},
                            device_id_type=MESH,
                        ).wait_recv()

        for copy in copies:
            copy.wait()

    def result(m, g, v):
        shape = v.shape
        if m == "share":
            shape = (size_of(g),) + shape
        elif m == "expert":
            shape = (8, 128, 256)
        return jax.ShapeDtypeStruct(shape, v.dtype)

    spec = pl.BlockSpec(memory_space=pltpu.VMEM)
    far = pl.BlockSpec(memory_space=pl.ANY)
    return pl.pallas_call(
        kernel,
        out_shape=[result(m, g, v) for m, g, v in items],
        in_specs=[far if m == "expert" else spec for m in modes],
        out_specs=[spec] * count,
        scratch_shapes=[
            pltpu.SemaphoreType.DMA((count, most)),
            pltpu.SemaphoreType.DMA((count, most)),
            pltpu.SemaphoreType.DMA((count,)),
        ],
        compiler_params=pltpu.CompilerParams(
            collective_id=number, has_side_effects=True, vmem_limit_bytes=60 * 1024 * 1024
        ),
        name=f"exchange{number}",
    )(*arrays)


def expert_kernel(
    sent_x, sent_top, sent_p, near0, near1, near2,
    returned, gains_back, scaled0, scaled1, total,
    slots_x, slots_top, slots_p, far0, far1, far2, pulled, gains,
    gate_w, up_w, down_w, rows_in, rows_top, hidden_s, gate_s, up_s, out_s, gate_g, up_g,
    block_s, kept, given, other,
    send, recv, send_back, recv_back, send_core, recv_core, local,
):
    dp, z, c = (lax.axis_index(a) for a in AXES)
    x, core = (dp // 2) % 4, dp % 2
    me = member(PLANE)
    near, far = (near0, near1, near2), (far0, far1, far2)
    barrier = pltpu.get_barrier_semaphore()
    steps = steps_of(PLANE)
    mate = goal((CORE,), (1,))[1]
    for move in steps:
        pl.semaphore_signal(
            barrier, inc=1, device_id=goal(PLANE, move)[1], device_id_type=MESH
        )
    pl.semaphore_signal(barrier, inc=1, device_id=mate, device_id_type=MESH)
    pl.semaphore_wait(barrier, len(steps) + 1)

    def to_mate(source, target, k):
        return pltpu.make_async_remote_copy(
            src_ref=source,
            dst_ref=target,
            send_sem=send_core.at[k],
            recv_sem=recv_core.at[k],
            device_id=mate,
            device_id_type=MESH,
        )

    swaps = [to_mate(near[i], far[i], 8 + i) for i in range(3)]
    for copy in swaps:
        copy.start()
    out_going = []
    for k, (source, target) in enumerate(
        ((sent_x, slots_x), (sent_p, slots_p), (sent_top, slots_top))
    ):
        group = []
        for i, move in enumerate(steps):
            index, place = goal(PLANE, move)
            group.append(
                pltpu.make_async_remote_copy(
                    src_ref=source.at[index],
                    dst_ref=target.at[me],
                    send_sem=send.at[k, i],
                    recv_sem=recv.at[k, i],
                    device_id=place,
                    device_id_type=MESH,
                )
            )
            group[-1].start()
        group.append(pltpu.make_async_copy(source.at[me], target.at[me], local.at[k]))
        group[-1].start()
        out_going.append(group)

    for copy in swaps:
        copy.wait()
    for which in range(3):
        for zs in range(4):
            for cs in range(2):
                for half in range(2):
                    part = jnp.where(
                        core == half, near[which][zs + 4 * cs], far[which][zs + 4 * cs]
                    )
                    if which < 2:
                        (gate_w, up_w)[which][
                            zs * 256 + half * 128 : zs * 256 + half * 128 + 128,
                            cs * 256 : cs * 256 + 256,
                        ] = part
                    else:
                        down_w[
                            cs * 256 + half * 128 : cs * 256 + half * 128 + 128,
                            zs * 256 : zs * 256 + 256,
                        ] = part
    for copy in out_going[0]:
        copy.wait()

    def forward(s, _):
        span = pl.ds(pl.multiple_of(s * CAP, CAP), CAP)
        x_rows = jnp.concatenate([slots_x[4 * s + j] for j in range(4)], axis=1)
        gate_act = dot(x_rows, gate_w[...], ((1,), (0,)))
        up_act = dot(x_rows, up_w[...], ((1,), (0,)))
        hidden = (gate_act * jax.nn.sigmoid(gate_act) * up_act).astype(LOW)
        out_s[span, :] = dot(hidden, down_w[...], ((1,), (0,)))
        rows_in[span, :] = x_rows
        hidden_s[span, :] = hidden
        gate_s[span, :] = gate_act
        up_s[span, :] = up_act
        return 0

    lax.fori_loop(0, 4, forward, 0)
    for copy in out_going[1] + out_going[2]:
        copy.wait()

    def home_of(s, j):
        place = {"dp": dp + 2 * (s - x), "row": j, "col": c}
        return place, 4 * s + j

    def go_back(s, j, from_x, from_g):
        place, index = home_of(s, j)
        return [
            pltpu.make_async_remote_copy(
                src_ref=source,
                dst_ref=target.at[me],
                send_sem=send_back.at[k, index],
                recv_sem=recv_back.at[k, me],
                device_id=place,
                device_id_type=MESH,
            )
            for k, (source, target) in enumerate(((from_x, returned), (from_g, gains_back)))
        ]

    def backward(i, _):
        s = (x + 2 + i) % 4
        span = pl.ds(pl.multiple_of(s * CAP, CAP), CAP)
        top = jnp.concatenate([slots_top[4 * s + j] for j in range(4)], axis=1).astype(F32)
        p = jnp.transpose(slots_p[4 * s])[:CAP, :1]
        gate_act, up_act, out = gate_s[span, :], up_s[span, :], out_s[span, :]
        sig = jax.nn.sigmoid(gate_act)
        slot_grad = (p * top).astype(LOW)
        hidden_grad = dot(slot_grad, down_w[...], ((1,), (1,)))
        grad_gate = (hidden_grad * up_act * sig * (1.0 + gate_act * (1.0 - sig))).astype(LOW)
        grad_up = (hidden_grad * gate_act * sig).astype(LOW)
        pull = dot(grad_gate, gate_w[...], ((1,), (1,)))
        pull = (pull + dot(grad_up, up_w[...], ((1,), (1,)))).astype(LOW)
        gain = jnp.sum(top * out, axis=1, keepdims=True)
        gains[s] = jnp.zeros((8, 256), F32)
        gains[s, :, :CAP] = jnp.transpose(jnp.broadcast_to(gain, (CAP, 128)))[:8]
        for j in range(4):
            pulled[j, s] = pull[:, j * 256 : j * 256 + 256]
        rows_top[span, :] = slot_grad
        gate_g[span, :] = grad_gate
        up_g[span, :] = grad_up
        out = (p * out).astype(LOW)
        for j in range(4):
            scaled0[4 * s + j] = out[: CAP // 2, j * 256 : j * 256 + 256]
            scaled1[4 * s + j] = out[CAP // 2 :, j * 256 : j * 256 + 256]
        for kz in (2, 1, 3, 0):
            j = (z + kz) % 4

            @pl.when((s != x) | (j != z))
            def _(j=j):
                for copy in go_back(s, j, pulled.at[j, s], gains.at[s]):
                    copy.start()

        return 0

    lax.fori_loop(0, 4, backward, 0)
    near_rows = pl.ds(pl.multiple_of(core * 128, 128), 128)
    far_rows = pl.ds(pl.multiple_of((1 - core) * 128, 128), 128)

    def block(m, _):
        wide = pl.ds(pl.multiple_of((m % 4) * 256, 256), 256)
        narrow = pl.ds(pl.multiple_of((m // 4) * 256, 256), 256)
        for which in range(3):
            if which < 2:
                left, right = rows_in[:, wide], (gate_g, up_g)[which][:, narrow]
            else:
                left, right = hidden_s[:, narrow], rows_top[:, wide]
            block_s[...] = dot(left, right, ((0,), (0,)))
            given[m, which] = block_s[far_rows, :].astype(LOW)
            kept[m, which] = block_s[near_rows, :]
        to_mate(given.at[m], other.at[m], m).start()
        return 0

    lax.fori_loop(0, 8, block, 0)
    returned[me] = pulled[z, x]
    gains_back[me] = gains[x]

    def add(m, _):
        to_mate(given.at[m], other.at[m], m).wait()
        total[m] = (kept[m] + other[m].astype(F32)).astype(LOW)
        return 0

    lax.fori_loop(0, 8, add, 0)
    for move in steps:
        index, place = goal(PLANE, move)
        for k, (source, target) in enumerate(
            ((pulled.at[0, 0], returned), (gains.at[0], gains_back))
        ):
            copy = pltpu.make_async_remote_copy(
                src_ref=source,
                dst_ref=target.at[index],
                send_sem=send_back.at[k, index],
                recv_sem=recv_back.at[k, index],
                device_id=place,
                device_id_type=MESH,
            )
            copy.wait_send()
            copy.wait_recv()


def expert_step(number, *operands):
    spec = pl.BlockSpec(memory_space=pltpu.VMEM)
    rows_of = jax.ShapeDtypeStruct((16, CAP, 256), LOW)
    return pl.pallas_call(
        expert_kernel,
        out_shape=[
            rows_of,
            jax.ShapeDtypeStruct((16, 8, 256), F32),
            jax.ShapeDtypeStruct((16, CAP // 2, 256), LOW),
            jax.ShapeDtypeStruct((16, CAP // 2, 256), LOW),
            jax.ShapeDtypeStruct((8, 3, 128, 256), LOW),
        ],
        in_specs=[spec] * 6,
        out_specs=[spec] * 5,
        scratch_shapes=[
            pltpu.VMEM((16, CAP, 256), LOW),
            pltpu.VMEM((16, CAP, 256), LOW),
            pltpu.VMEM((16, 8, 256), F32),
            pltpu.VMEM((8, 128, 256), LOW),
            pltpu.VMEM((8, 128, 256), LOW),
            pltpu.VMEM((8, 128, 256), LOW),
            pltpu.VMEM((4, 4, CAP, 256), LOW),
            pltpu.VMEM((4, 8, 256), F32),
            pltpu.VMEM((D, 512), LOW),
            pltpu.VMEM((D, 512), LOW),
            pltpu.VMEM((512, D), LOW),
            pltpu.VMEM((640, D), LOW),
            pltpu.VMEM((640, D), LOW),
            pltpu.VMEM((640, 512), LOW),
            pltpu.VMEM((640, 512), F32),
            pltpu.VMEM((640, 512), F32),
            pltpu.VMEM((640, D), F32),
            pltpu.VMEM((640, 512), LOW),
            pltpu.VMEM((640, 512), LOW),
            pltpu.VMEM((256, 256), F32),
            pltpu.VMEM((8, 3, 128, 256), F32),
            pltpu.VMEM((8, 3, 128, 256), LOW),
            pltpu.VMEM((8, 3, 128, 256), LOW),
            pltpu.SemaphoreType.DMA((3, 15)),
            pltpu.SemaphoreType.DMA((3, 15)),
            pltpu.SemaphoreType.DMA((2, 16)),
            pltpu.SemaphoreType.DMA((2, 16)),
            pltpu.SemaphoreType.DMA((11,)),
            pltpu.SemaphoreType.DMA((11,)),
            pltpu.SemaphoreType.DMA((3,)),
        ],
        compiler_params=pltpu.CompilerParams(
            collective_id=number, has_side_effects=True, vmem_limit_bytes=60 * 1024 * 1024
        ),
        name="expert",
    )(*operands)


TAIL_OUT = (
    ((8, 3, 128, 256), LOW),
    ((16, 32, 256), LOW),
    ((16, 8, 256), F32),
    ((16, 16, 1024), LOW),
    ((16, 8, 256), F32),
    ((512, 256), LOW),
    ((512, 256), LOW),
)
TAIL_SCRATCH = (
    ((512, 256), LOW),
    ((2, 16, 512), F32),
    ((8, 8, 512), F32),
    ((4, 32, 512), F32),
    ((4, 128, 256), LOW),
    ((16, 80, 256), LOW),
    ((16, 80, 256), LOW),
    ((512, 256), LOW),
    ((4, 512, 256), LOW),
    ((512, 256), F32),
    ((512, 256), LOW),
    ((16, 32, 256), LOW),
    ((32, 256), LOW),
    ((16, 8, 256), F32),
    ((16, 8, 256), F32),
    ((8, 256), F32),
    ((512, 256), LOW),
    ((4, 512, 256), LOW),
    ((512, 1024), LOW),
    ((512, 256), LOW),
    ((512, 256), LOW),
    ((8, 512), F32),
    ((8, 8, 512), F32),
    ((256, 1024), LOW),
    ((16, 16, 1024), LOW),
    ((16, 1024), LOW),
    ((8, 256), F32),
    ((512, 256), F32),
    ((512, 256), LOW),
    ((512, 256), LOW),
)
TAIL_SEMS = 224


def as_row(column):
    return jnp.transpose(jnp.broadcast_to(column, (512, 128)))[:8]


def as_column(row):
    return jnp.transpose(jnp.broadcast_to(row, (8, 512)))[:, :1]


def tail_kernel(
    home_ref, gain_own_ref, pull_ref, router_gain_ref, w_out_ref, scaled0_ref, scaled1_ref,
    kept_ref, resid_mid_ref, cot_ref, scale_ffn_ref, gain2_ref, probs_ref, router_ref,
    normed_ffn_ref, attended_all_ref, attended_ref, queries_ref, keys_ref, values_ref,
    weights_ref, cos_q_ref, sin_q_ref, cos_kv_ref, sin_kv_ref, whole_ref, normed_own_ref,
    x_in_ref, scale_attn_ref, gain1_ref, own_rank_ref, owned_ref, out_sum_ref,
    router_sum_ref, joined_sum_ref, gains_ref, block_out_ref, grad_input_ref, home2_ref,
    gain_pair_ref, pulls_ref, router_pull_ref, out_heads_ref, back0_ref, back1_ref, mid_ref,
    mid_all_ref, grad_mid_ref, g_out_ref, out_parts_ref, out_chunk_ref, g_router_ref,
    router_parts_ref, router_chunk_ref, proj_ref, proj_all_ref, flat_ref, gn_ref, gn2_ref,
    pull2_ref, pulls2_ref, g_joined_ref, joined_parts_ref, joined_chunk_ref, gains_own_ref,
    moe_sum_ref, moe_ref, moe2_ref, send, recv,
):
    dp, z, c = (lax.axis_index(a) for a in AXES)
    y_hi, x, core = dp // 8, (dp // 2) % 4, dp % 2
    owner = c * 8 + x * 2 + z // 2
    slot = (z % 2) * 4 + y_hi * 2 + core
    barrier = pltpu.get_barrier_semaphore()
    moves = {}
    for g in (TEAM, PLANE, ALL_DP):
        for move in steps_of(g):
            full = {d: k for d, k in zip(g, move) if k}
            moves[tuple(sorted(full.items()))] = (g, move)
    for g, move in moves.values():
        pl.semaphore_signal(barrier, inc=1, device_id=goal(g, move)[1], device_id_type=MESH)
    sources = []
    for i in range(8):
        place = {
            "dp": ((i // 2) % 2) * 8 + x * 2 + i % 2,
            "row": core * 2 + i // 4,
            "col": y_hi,
        }
        mine = (place["dp"] == dp) & (place["row"] == z) & (place["col"] == c)
        sources.append(mine)

        @pl.when(jnp.logical_not(mine))
        def _(place=place):
            pl.semaphore_signal(barrier, inc=1, device_id=place, device_id_type=MESH)

    @pl.when(owner == dp)
    def _():
        pl.semaphore_wait(barrier, len(moves) + 7)

    @pl.when(owner != dp)
    def _():
        pl.semaphore_wait(barrier, len(moves) + 8)

    used = [0]

    def begin(mode, group, source, target):
        me = member(group)
        copies = []
        for move in steps_of(group):
            index, place = goal(group, move)
            copies.append(
                pltpu.make_async_remote_copy(
                    src_ref=source(index) if mode == "split" else source,
                    dst_ref=target if mode == "swap" else target.at[me],
                    send_sem=send.at[used[0]],
                    recv_sem=recv.at[used[0]],
                    device_id=place,
                    device_id_type=MESH,
                )
            )
            used[0] += 1
            copies[-1].start()
        if mode != "swap":
            target[me] = source(me)[...] if mode == "split" else source[...]
        return copies

    def wait(copies):
        for copy in copies:
            copy.wait()

    kept, owned = kept_ref, owned_ref
    first_deliver = TAIL_SEMS - 24

    def parcel(which, j, to_slot):
        return pltpu.make_async_remote_copy(
            src_ref=kept.at[j, which],
            dst_ref=owned.at[to_slot, which],
            send_sem=send.at[first_deliver + which * 8 + j],
            recv_sem=recv.at[first_deliver + which * 8 + to_slot],
            device_id={"dp": owner, "row": j % 4, "col": j // 4},
            device_id_type=MESH,
        )

    def own(j):
        return (owner == dp) & (z == j % 4) & (c == j // 4)

    def deliver(which):
        for kz, kc in ((2, 1), (2, 0), (1, 1), (3, 1), (1, 0), (3, 0), (0, 1), (0, 0)):
            j = (z + kz) % 4 + 4 * ((c + kc) % 2)

            @pl.when(own(j))
            def _(j=j):
                owned[slot, which] = kept[j, which]

            @pl.when(jnp.logical_not(own(j)))
            def _(j=j):
                parcel(which, j, slot).start()

    first = begin("swap", (SIDE,), home_ref, home2_ref)
    first += begin("share", (SIDE,), gain_own_ref, gain_pair_ref)
    first += begin("share", TEAM, pull_ref, pulls_ref)
    first += begin("share", (Z,), router_gain_ref, router_pull_ref)
    heads = begin("split", (Z,), lambda j: w_out_ref.at[j], out_heads_ref)
    back0 = begin("split", PLANE, lambda j: scaled0_ref.at[j], back0_ref)
    wait(first)
    home = home_ref[...].astype(F32) + home2_ref[...].astype(F32)
    grad_prob = jnp.concatenate([gain_pair_ref[0], gain_pair_ref[1]], axis=0)
    probs = probs_ref[...]
    inner = jnp.sum(probs * grad_prob, axis=0, keepdims=True)
    grad_logits = (probs * (grad_prob - inner)).astype(LOW)
    router_pull = (router_pull_ref[0] + router_pull_ref[1]) + (
        router_pull_ref[2] + router_pull_ref[3]
    )
    row = jnp.sum(grad_logits.astype(F32) * router_pull, axis=0, keepdims=True)
    for i in range(8):
        row = row + pulls_ref[i, :1]
    project = as_column(row) / D
    grad_normed = home + dot(grad_logits, router_ref[...], ((0,), (0,)))
    resid_mid, scale = resid_mid_ref[...], scale_ffn_ref[...]
    weighted = grad_normed * gain2_ref[...]
    grad_mid = (
        cot_ref[...].astype(F32) + scale * weighted - resid_mid * scale**3 * project
    )
    mid_ref[...] = grad_mid.astype(LOW)
    grad_mid_ref[...] = grad_mid
    gains_own_ref[...] = jnp.zeros((8, 256), F32)
    gains_own_ref[1:2] = jnp.sum(grad_normed * resid_mid * scale, axis=0, keepdims=True)
    middle = begin("share", (Z,), mid_ref, mid_all_ref)
    grad_router = dot(grad_logits, normed_ffn_ref[...], ((1,), (0,)))
    g_router_ref[...] = jnp.zeros((16, 8, 256), F32)
    for j in range(16):
        g_router_ref[j, :2] = grad_router[2 * j : 2 * j + 2]
    for j in range(4):
        g_out_ref[j * 128 : j * 128 + 128] = dot(
            attended_all_ref[4 * c + j], mid_ref[...], ((0,), (0,))
        ).astype(LOW)
    sums = begin(
        "split",
        ALL_DP,
        lambda j: g_out_ref.at[pl.ds(pl.multiple_of(j * 32, 32), 32)],
        out_parts_ref,
    )
    sums += begin("split", ALL_DP, lambda j: g_router_ref.at[j], router_parts_ref)
    deliver(0)

    wait(heads)
    wait(middle)
    grad_att = dot(mid_all_ref[0], out_heads_ref[0], ((1,), (1,)))
    for j in range(1, 4):
        grad_att = grad_att + dot(mid_all_ref[j], out_heads_ref[j], ((1,), (1,)))
    grad_att = grad_att.astype(LOW)
    product = grad_att.astype(F32) * attended_ref[...].astype(F32)
    keys, values = keys_ref[...], values_ref[...]
    grad_q = []
    grad_k = jnp.zeros((512, HEAD_DIM), F32)
    grad_v = jnp.zeros((512, HEAD_DIM), F32)
    for h in range(2):
        span = slice(h * HEAD_DIM, h * HEAD_DIM + HEAD_DIM)
        grad_h = grad_att[:, span]
        weights = weights_ref[h]
        delta = jnp.sum(product[:, span], axis=1, keepdims=True)
        grad_weights = dot(grad_h, values, ((1,), (1,)))
        grad_scores = (weights * (grad_weights - delta)).astype(LOW)
        grad_q.append(dot(grad_scores, keys, ((1,), (0,))))
        grad_k = grad_k + dot(grad_scores, queries_ref[:, span], ((0,), (0,)))
        grad_v = grad_v + dot(weights.astype(LOW), grad_h, ((0,), (0,)))
    score_scale = HEAD_DIM ** (-0.5)
    low_lane = lax.broadcasted_iota(jnp.int32, (512, 128), 1) % 64 < 32

    def turn(value, cosine, sine_part):
        other = jnp.where(low_lane, pltpu.roll(value, 96, 1), pltpu.roll(value, 32, 1))
        return (value * cosine + other * sine_part).astype(LOW)

    both = jnp.concatenate(grad_q, axis=1) * score_scale
    proj_ref[:, :128] = turn(both, cos_q_ref[...], sin_q_ref[...])
    both = jnp.concatenate([grad_k * score_scale, grad_v], axis=1)
    proj_ref[:, 128:] = turn(both, cos_kv_ref[...], sin_kv_ref[...])
    projected = begin("share", (Z,), proj_ref, proj_all_ref)
    back1 = begin("split", PLANE, lambda j: scaled1_ref.at[j], back1_ref)

    wait(sums)
    total = out_parts_ref[0].astype(F32)
    routed = router_parts_ref[0]
    for j in range(1, 16):
        total = total + out_parts_ref[j].astype(F32)
        routed = routed + router_parts_ref[j]
    out_chunk_ref[...] = total.astype(LOW)
    router_chunk_ref[...] = routed
    rest = begin("share", ALL_DP, out_chunk_ref, out_sum_ref)
    rest += begin("share", ALL_DP, router_chunk_ref, router_sum_ref)
    moe_sum_ref[...] = jnp.zeros((512, 256), F32)

    def add_half(rows_of, start):
        def one(e, _):
            places = lax.broadcasted_iota(jnp.int32, (80, 512), 0) + start
            taken = (own_rank_ref[e] == places).astype(F32).astype(LOW)
            moe_sum_ref[...] += dot(taken, rows_of[e], ((0,), (0,)))
            return 0

        lax.fori_loop(0, 16, one, 0)

    wait(back0)
    add_half(back0_ref, 0)

    wait(projected)
    for j in range(4):
        flat_ref[:, j * 128 : j * 128 + 128] = proj_all_ref[j, :, :128]
        flat_ref[:, 512 + j * 64 : 576 + j * 64] = proj_all_ref[j, :, 128:192]
        flat_ref[:, 768 + j * 64 : 832 + j * 64] = proj_all_ref[j, :, 192:]
    grad_low = dot(flat_ref[...], whole_ref[...], ((1,), (1,))).astype(LOW)
    residual, gain1 = x_in_ref[...].astype(F32), gain1_ref[...]
    gn_ref[...] = grad_low
    pull = jnp.sum(grad_low.astype(F32) * gain1 * residual, axis=1, keepdims=True)
    pull2_ref[...] = as_row(pull)
    meet = begin("swap", (SIDE,), gn_ref, gn2_ref)
    meet += begin("share", TEAM, pull2_ref, pulls2_ref)
    g_joined_ref[...] = dot(normed_own_ref[...], flat_ref[...], ((0,), (0,))).astype(LOW)
    joined = begin(
        "split",
        ALL_DP,
        lambda j: g_joined_ref.at[pl.ds(pl.multiple_of(j * 16, 16), 16)],
        joined_parts_ref,
    )
    deliver(1)
    wait(back1)
    add_half(back1_ref, 80)
    moe_ref[...] = moe_sum_ref[...].astype(LOW)
    moe = begin("swap", (SIDE,), moe_ref, moe2_ref)
    wait(meet)
    grad_normed = gn_ref[...].astype(F32) + gn2_ref[...].astype(F32)
    row = pulls2_ref[0, :1]
    for i in range(1, 8):
        row = row + pulls2_ref[i, :1]
    project = as_column(row) / D
    weighted = grad_normed * gain1
    scale = scale_attn_ref[...]
    grad_input_ref[...] = (
        grad_mid_ref[...] + scale * weighted - residual * scale**3 * project
    ).astype(LOW)
    gains_own_ref[0:1] = jnp.sum(grad_normed * residual * scale, axis=0, keepdims=True)
    wait(joined)
    total = joined_parts_ref[0].astype(F32)
    for j in range(1, 16):
        total = total + joined_parts_ref[j].astype(F32)
    joined_chunk_ref[...] = total.astype(LOW)
    rest += begin("share", ALL_DP, joined_chunk_ref, joined_sum_ref)
    rest += begin("share", ALL_DP, gains_own_ref, gains_ref)
    deliver(2)
    wait(moe)
    block_out_ref[...] = (
        resid_mid + (moe_ref[...].astype(F32) + moe2_ref[...].astype(F32))
    ).astype(LOW)
    wait(rest)
    for which in range(3):
        for j in range(8):

            @pl.when(jnp.logical_not(own(j)))
            def _(j=j, which=which):
                parcel(which, j, slot).wait_send()

            @pl.when(jnp.logical_not(sources[j]))
            def _(j=j, which=which):
                parcel(which, 0, j).wait_recv()


def tail_step(number, *operands):
    spec = pl.BlockSpec(memory_space=pltpu.VMEM)
    return pl.pallas_call(
        tail_kernel,
        out_shape=[jax.ShapeDtypeStruct(*v) for v in TAIL_OUT],
        in_specs=[spec] * len(operands),
        out_specs=[spec] * len(TAIL_OUT),
        scratch_shapes=[pltpu.VMEM(*v) for v in TAIL_SCRATCH]
        + [pltpu.SemaphoreType.DMA((TAIL_SEMS,)), pltpu.SemaphoreType.DMA((TAIL_SEMS,))],
        compiler_params=pltpu.CompilerParams(
            collective_id=number, has_side_effects=True, vmem_limit_bytes=60 * 1024 * 1024
        ),
        name="tail",
    )(*operands)


def rope_tables(positions):
    half_dim = HEAD_DIM // 2
    exponent = jnp.arange(half_dim).astype(F32) * (2.0 / HEAD_DIM)
    angles = positions.astype(F32)[:, None] * (ROPE_BASE ** (-exponent))[None, :]
    return (jnp.cos(angles)[:, None, :], jnp.sin(angles)[:, None, :])


def rotate(values_in, cosine, sine_part):
    half_dim = values_in.shape[-1] // 2
    low_half = values_in[..., :half_dim]
    high_half = values_in[..., half_dim:]
    return jnp.concatenate(
        [low_half * cosine - high_half * sine_part, high_half * cosine + low_half * sine_part],
        axis=-1,
    )


def dot(a, b, dims):
    return lax.dot_general(a, b, (dims, ((), ())), preferred_element_type=F32)


def rows(vector):
    return vector.reshape(4, 128)


def on_device(
    x_in,
    segments,
    expert_ids,
    cotangent,
    norm_gain1,
    w_query,
    w_key,
    w_value,
    w_out,
    norm_gain2,
    w_router,
    w_gate,
    w_up,
    w_down,
):
    dp, z, c = (lax.axis_index(a) for a in ("dp", "row", "col"))
    score_scale = HEAD_DIM ** (-0.5)

    joined = jnp.concatenate(
        [
            w_query.reshape(256, 4, 128),
            w_key.reshape(256, 4, 64),
            w_value.reshape(256, 4, 64),
        ],
        axis=2,
    )
    x_all, head_weights, gain_all, out_all = exchange(
        2,
        ("share", (Z,), x_in),
        ("split", (Z,), joined.transpose(1, 0, 2)),
        ("share", (Z,), norm_gain1.reshape(2, 128)),
        ("share", (SIDE,), w_out),
    )
    out_all = out_all.reshape(1024, 256)
    residual_all = x_all.astype(F32)
    scale_attn = lax.rsqrt(jnp.sum(residual_all * residual_all, axis=(0, 2)) / D + EPSILON)[
        :, None
    ]
    normed_all = (residual_all * scale_attn[None] * gain_all.reshape(4, 1, 256)).astype(LOW)
    normed_flat = normed_all.transpose(1, 0, 2).reshape(LENGTH, D)
    projected = dot(normed_flat, head_weights.reshape(D, 256), ((1,), (0,)))
    cosine, sine_part = rope_tables(jnp.arange(LENGTH, dtype=jnp.int32))
    queries = rotate(projected[:, :128].reshape(LENGTH, 2, HEAD_DIM), cosine, sine_part)
    queries = queries.astype(LOW)
    keys = rotate(projected[:, 128:192].reshape(LENGTH, 1, HEAD_DIM), cosine, sine_part)
    keys = keys.astype(LOW)[:, 0]
    values = projected[:, 192:].astype(LOW)
    places = jnp.arange(LENGTH, dtype=jnp.int32)
    segment_row = segments.reshape(-1)
    allowed = (places[None, :] <= places[:, None]) & (
        segment_row[None, :] == segment_row[:, None]
    )
    scores = jnp.einsum("qhd,kd->hqk", queries, keys, preferred_element_type=F32) * score_scale
    scores = jnp.where(allowed[None], scores, MASKED)
    top_score = jnp.max(scores, axis=2, keepdims=True)
    log_total = top_score + jnp.log(jnp.sum(jnp.exp(scores - top_score), axis=2, keepdims=True))
    weights = jnp.exp(scores - log_total)
    weights_low = weights.astype(LOW)
    attended = jnp.einsum("hqk,kd->qhd", weights_low, values, preferred_element_type=F32)
    attended = attended.astype(LOW).reshape(LENGTH, 128)

    attended_all, near_gate = exchange(
        4, ("share", TEAM, attended), ("expert", TEAM, w_gate)
    )
    attended_flat = attended_all.transpose(1, 0, 2).reshape(LENGTH, 1024)
    residual = x_in.astype(F32)
    resid_mid = residual + dot(attended_flat, out_all, ((1,), (0,)))
    square_parts, near_up = exchange(
        5,
        ("share", (Z,), rows(jnp.sum(resid_mid * resid_mid, axis=1))),
        ("expert", TEAM, w_up),
    )
    squares = jnp.sum(square_parts, axis=0).reshape(LENGTH)
    scale_ffn = lax.rsqrt(squares / D + EPSILON)[:, None]
    normed_ffn = (resid_mid * scale_ffn * norm_gain2).astype(LOW)
    router = w_router.T
    router_gain = lax.dot_general(
        router.astype(F32),
        resid_mid * norm_gain2,
        (((1,), (1,)), ((), ())),
        precision=lax.Precision.HIGHEST,
        preferred_element_type=F32,
    )
    logit_parts, near_down = exchange(
        6,
        ("share", (Z,), dot(router, normed_ffn, ((1,), (1,)))),
        ("expert", TEAM, w_down),
    )
    logits = jnp.sum(logit_parts, axis=0)

    experts = jnp.arange(EXPERTS, dtype=jnp.int32)[:, None]
    hits = jnp.any(expert_ids.T[None, :, :] == experts[:, :, None], axis=1)
    chosen = jnp.where(hits, logits, MASKED)
    chosen = jnp.where(hits, jnp.exp(chosen - jnp.max(chosen, axis=0, keepdims=True)), 0.0)
    probs = chosen / jnp.sum(chosen, axis=0, keepdims=True)
    earlier = (places[:, None] < places[None, :]).astype(LOW)
    rank = dot(hits.astype(LOW), earlier, ((1,), (0,)))
    rank = jnp.where(hits, rank, -1.0).astype(jnp.int32)
    own_rank = lax.dynamic_slice(rank, (c * 16, 0), (16, LENGTH))
    own_probs = lax.dynamic_slice(probs, (c * 16, 0), (16, LENGTH))
    taken = own_rank[:, None, :] == jnp.arange(CAP, dtype=jnp.int32)[None, :, None]
    pick = taken.astype(LOW)
    sent_x = jnp.einsum("est,td->esd", pick, normed_ffn, preferred_element_type=F32)
    sent_top = jnp.einsum("est,td->esd", pick, cotangent, preferred_element_type=F32)
    slot_probs = jnp.sum(jnp.where(taken, own_probs[:, None, :], 0.0), axis=2)
    slot_probs = jnp.pad(slot_probs, ((0, 0), (0, 96)))
    slot_probs = jnp.broadcast_to(slot_probs[:, None, :], (16, 8, 256))
    pulled, gain_rows, scaled0, scaled1, kept = expert_step(
        7, sent_x.astype(LOW), sent_top.astype(LOW), slot_probs, near_gate, near_up, near_down
    )

    home = jnp.einsum("est,esd->td", pick, pulled, preferred_element_type=F32).astype(LOW)
    gain_rows = gain_rows[:, 0, :CAP]
    own_gain = jnp.sum(jnp.where(taken, gain_rows[:, :, None], 0.0), axis=1)
    pull = jnp.sum(home.astype(F32) * norm_gain2 * resid_mid, axis=1)
    cos_part, sin_part = cosine[:, 0], sine_part[:, 0]
    idle = jnp.zeros((LENGTH, HEAD_DIM), F32)
    owned, out_sum, router_sum, joined_sum, gains, block_out, grad_input = tail_step(
        11,
        home,
        own_gain,
        jnp.broadcast_to(pull[None], (8, LENGTH)),
        router_gain,
        w_out.reshape(4, 128, 256),
        scaled0,
        scaled1,
        kept,
        resid_mid,
        cotangent,
        scale_ffn,
        norm_gain2.reshape(1, 256),
        probs,
        router,
        normed_ffn,
        attended_all,
        attended,
        queries.reshape(LENGTH, 128),
        keys,
        values,
        weights,
        jnp.concatenate([cos_part] * 4, axis=1),
        jnp.concatenate([sin_part, -sin_part] * 2, axis=1),
        jnp.concatenate([cos_part, cos_part, idle + 1.0], axis=1),
        jnp.concatenate([sin_part, -sin_part, idle], axis=1),
        jnp.concatenate([w_query, w_key, w_value], axis=1),
        (residual * scale_attn * norm_gain1).astype(LOW),
        x_in,
        scale_attn,
        norm_gain1.reshape(1, 256),
        own_rank.reshape(16, 1, LENGTH),
    )
    joined_sum = joined_sum.reshape(256, 1024).astype(F32)
    gain_sum = jnp.sum(gains, axis=0)
    owned = jnp.sum(owned.astype(F32).reshape(2, 2, 2, 3, 128, 256), axis=1)
    owned = owned.transpose(2, 0, 1, 3, 4).reshape(3, 2, 256, 256)
    return (
        block_out,
        grad_input,
        joined_sum[:, :512],
        joined_sum[:, 512:768],
        joined_sum[:, 768:],
        out_sum.reshape(512, 256).astype(F32),
        router_sum[:, :2].reshape(EXPERTS, 256).T,
        owned[0],
        owned[1],
        owned[2],
        gain_sum[0],
        gain_sum[1],
    )


def solution(mesh):
    placed = (
        P("dp", "row"),
        P("dp", None),
        P("dp", None),
        P("dp", "row"),
        P("row"),
        P("row", "col"),
        P("row", "col"),
        P("row", "col"),
        P("col", "row"),
        P("row"),
        P("row", None),
        P(None, "row", "col"),
        P(None, "row", "col"),
        P(None, "col", "row"),
    )
    return jax.shard_map(
        on_device,
        mesh=mesh,
        in_specs=placed,
        out_specs=(
            P("dp", "row"),
            P("dp", "row"),
            P("row", "col"),
            P("row", "col"),
            P("row", "col"),
            P("col", "row"),
            P("row", None),
            P("dp", "row", "col"),
            P("dp", "row", "col"),
            P("dp", "col", "row"),
            P("row"),
            P("row"),
        ),
        check_vma=False,
    )
```

time: 1190 us -> 301 us (0.25)
  waiting for transfers between devices: 751 us -> 0 us
  Pallas kernels: 0 us -> 248 us
  blocking collectives: 147 us -> 0 us
  local copies, waits for them, and re-layouts: 157 us -> 20.1 us
  matrix products: 66.9 us -> 14 us
  other arithmetic: 44.7 us -> 17.2 us
  between operations: 14.9 us -> 1.12 us
    reduce_scatter x7 -> x0, waiting for transfers between devices: 458 us -> none  [the longest x2 158 us: slot_share(): return lax.psum_scatter(matrix, 'row', scatter_dimension=0, tiled=True)]
    pallas_call x0 -> x6, Pallas kernels: none -> 248 us  [the longest x1 109 us: tail_step(): pl.pallas_call(tail_kernel, out_shape=[jax.ShapeDtypeStruct(*v) for v in...]
    psum x5 -> x0, waiting for transfers between devices: 200 us -> none  [the longest x3 93.5 us: col_total(): return lax.psum(matrix, 'col')]
    psum x6 -> x0, blocking collectives: 126 us -> none  [the longest x1 64.4 us: on_device(): lax.psum((grad_joined, grad_out_part, grad_router, grad_gain1, grad_gain2...]
    gather x9 -> x0, local copies, waits for them, and re-layouts: 106 us -> none  [the longest x5 29.4 us: on_device(): jnp.take_along_axis(logits, expert_ids, axis=1)]
    all_gather x3 -> x0, waiting for transfers between devices: 93.5 us -> none  [the longest x2 66.9 us: slot_collect(): return lax.all_gather(matrix, 'row', axis=0, tiled=True)]
    dot_general x21 -> x10, matrix products: 66.9 us -> 14 us  [the longest x4 4.1 us: dot(): return lax.dot_general(a, b, (dims, ((), ())), preferred_element_type=F32)]
    all_gather x2 -> x0, blocking collectives: 21.2 us -> none  [head_collect(): return lax.all_gather(matrix, 'row', axis=0, tiled=True)]
  transfers between devices with their start and end apart: 15 -> 0, of which waited for: 15 -> 0; matrix products, arithmetic and copies ran while one was open for 9% -> 0% of each run, Pallas kernels for 0% -> 0%
where the time goes in v1:
time: 301 us
  Pallas kernels  248 us (82%)
  local copies, waits for them, and re-layouts  20.1 us (7%)
  other arithmetic  17.2 us (6%)
  matrix products  14 us (5%)
    pallas_call x1, Pallas kernels, tail_step(): pl.pallas_call(tail_kernel, out_shape=[jax.ShapeDtypeStruct(*v) for v in...  109 us
    pallas_call x4, Pallas kernels, exchange(): pl.pallas_call(kernel, out_shape=[result(m, g, v) for m, g, v in items],...  77 us
    pallas_call x1, Pallas kernels, expert_step(): pl.pallas_call(expert_kernel, out_shape=[rows_of, jax.ShapeDtypeStruct((1...  61.7 us

profile of v1, /device:TPU:1, one launch (start us, length us, event | category | flops | bytes accessed | tf_op | source)
XLA Modules:
  0.0 300.6 jit_solution(6523193878748364135)
XLA Ops:
  0.6 1.1 copy.96
  1.9 1.0 copy.97
  3.1 1.0 copy.98
  4.3 1.0 maximum_bitcast_fusion.refs_1_
  5.3 27.0 %exchange2.1 = (bf16[4,512,256]{2,1,0:T(8,128)(2,1)}, bf16[4,256,256]{2,1,0:T(8,128)(2,1)}, f32[4,2,128]{2,1,0:T(2,128)}, bf16[2,512,256]{2,1,0:T(8,128)(2,1)}) custom-call(bf16[512,256]{1,0:T(8,128)(2,1)} %x_in_ref.1, bf16[4,256,256]{2,1,0:T(8,128)(2,1)} %maximum_bitcast_fusion.refs_1_, f32[2,128]{1,0:T(2,128)} %bitcast.109, bf16[512,256]{1,0:T(8,128)(2,1)} %refs_3_.1), custom_call_target="tpu_custom_call" | custom-call | tf_op jit(solution)/shard_map/exchange2/pallas_call | solution.py:230
  32.2 1.5 fusion.6
  34.4 2.0 convolution_bitcast_fusion
  36.6 1.2 fusion.40
  38.0 1.0 fusion.41
  41.4 1.1 slice.72
  43.8 23.2 %exchange4.1 = (bf16[8,512,128]{2,1,0:T(8,128)(2,1)}, bf16[8,128,256]{2,1,0:T(8,128)(2,1)}) custom-call(bf16[512,128]{1,0:T(8,128)(2,1)} %copy.110.refs_0_.attended_ref, bf16[32,256,256]{2,1,0:T(8,128)(2,1)} %refs_1_.3), custom_call_target="tpu_custom_call" | custom-call | tf_op jit(solution)/shard_map/exchange4/pallas_call | solution.py:230
  67.0 1.6 copy.111
  68.6 1.1 multiply_reduce_fusion.1
  69.8 12.2 %exchange5.1 = (f32[4,4,128]{2,1,0:T(4,128)}, bf16[8,128,256]{2,1,0:T(8,128)(2,1)}) custom-call(f32[4,128]{1,0:T(4,128)} %bitcast.116, bf16[32,256,256]{2,1,0:T(8,128)(2,1)} %refs_1_.4), custom_call_target="tpu_custom_call" | custom-call | tf_op jit(solution)/shard_map/exchange5/pallas_call | solution.py:230
  83.7 14.7 %exchange6.1 = (f32[4,32,512]{2,1,0:T(8,128)}, bf16[8,128,256]{2,1,0:T(8,128)(2,1)}) custom-call(f32[32,512]{1,0:T(8,128)} %convolution_bitcast_fusion.1.refs_0_, bf16[32,256,256]{2,1,0:T(8,128)(2,1)} %refs_1_.5), custom_call_target="tpu_custom_call" | custom-call | tf_op jit(solution)/shard_map/exchange6/pallas_call | solution.py:230
  98.4 1.0 reduce_sum.103
  101.2 2.1 fusion.10.sent_top
  103.3 2.1 fusion.9.sent_x
  105.4 61.7 %expert.1 = (bf16[16,160,256]{2,1,0:T(8,128)(2,1)}, f32[16,8,256]{2,1,0:T(8,128)}, bf16[16,80,256]{2,1,0:T(8,128)(2,1)}, bf16[16,80,256]{2,1,0:T(8,128)(2,1)}, bf16[8,3,128,256]{3,2,1,0:T(8,128)(2,1)}) custom-call(bf16[16,160,256]{2,1,0:T(8,128)(2,1)} %fusion.9.sent_x, bf16[16,160,256]{2,1,0:T(8,128)(2,1)} %fusion.10.sent_top, ...), custom_call_target="tpu_custom_call" | custom-call | tf_op jit(solution)/shard_map/expert/pallas_call | solution.py:444
  167.0 0.9 slice.62
  168.0 2.1 select_reduce_fusion.gain_own_ref
  170.1 3.6 %multiply_reduce_fusion = (f32[512]{0:T(512)S(1)}, bf16[512,256]{1,0:T(8,128)(2,1)}) fusion(f32[512,256]{1,0:T(8,128)S(1)} %get-tuple-element.79.resid_mid_ref, f32[256]{0:T(256)S(1)} %copy-done.20, bf16[16,160,256]{2,1,0:T(8,128)(2,1)} %get-tuple-element.44, s32[16,512]{1,0:T(8,128)S(1)} %get-tuple-element.84), kind=kOutput, calls=%fused_computation.42 | convolution fusion | flops 673054208 | bytes 2132992 | tf_op jit(solution)/shard_map/est,esd->td/dot_general | solution.py:968
  175.0 0.9 copy.114.scale_ffn_ref
  175.8 1.0 convolution_bitcast_fusion.2.router_gain_ref
  177.7 1.4 fusion.32
  179.2 0.9 copy.117.scale_attn_ref
  180.0 0.8 fusion.21.normed_own_ref
  180.9 0.9 pad_maximum_fusion.whole_ref
  181.7 109.5 %tail.1 = (bf16[8,3,128,256]{3,2,1,0:T(8,128)(2,1)}, bf16[16,32,256]{2,1,0:T(8,128)(2,1)}, f32[16,8,256]{2,1,0:T(8,128)}, bf16[16,16,1024]{2,1,0:T(8,128)(2,1)},...) custom-call(bf16[512,256]{1,0:T(8,128)(2,1)} %get-tuple-element.81.home_ref, ...), custom_call_target="tpu_custom_call" | custom-call | tf_op jit(solution)/shard_map/tail/pallas_call | solution.py:817
  291.2 1.9 convert_reduce_fusion
  293.1 1.2 fusion.47
  297.0 0.9 slice.66
  (99 shorter events, 16.2 us)
Async XLA Ops:
  36.4 2.8 copy-start.11
  36.4 2.8 copy-start.21
  37.9 2.2 copy-start.6
  41.4 25.6 %copy-start = (f32[2,512,512]{2,1,0:T(8,128)}, f32[2,512,512]{2,1,0:T(8,128)S(1)}, u32[]{:S(2)}) copy-start(f32[2,512,512]{2,1,0:T(8,128)S(1)} %subtract_exponential_fusion.weights_ref) | copy-start | bytes 6291460
  42.6 24.4 %copy-start.4 = (bf16[512,64]{1,0:T(8,128)(2,1)}, bf16[512,64]{1,0:T(8,128)(2,1)S(1)}, u32[]{:S(2)}) copy-start(bf16[512,64]{1,0:T(8,128)(2,1)S(1)} %copy.124.values_ref) | copy-start | bytes 196612
  67.0 1.6 copy-start.2
  67.0 1.6 copy-start.22
  69.7 106.1 %copy-start.1 = (f32[512,256]{1,0:T(8,128)}, f32[512,256]{1,0:T(8,128)S(1)}, u32[]{:S(2)}) copy-start(f32[512,256]{1,0:T(8,128)S(1)} %get-tuple-element.79.resid_mid_ref) | copy-start | bytes 1572868
  69.7 13.0 %copy-start.20 = (f32[256]{0:T(256)S(1)}, f32[256]{0:T(256)}, u32[]{:S(2)}) copy-start(f32[256]{0:T(256)} %param.23) | copy-start | bytes 3076
  69.7 13.1 %copy-start.16 = (bf16[256,32]{0,1:T(8,128)(2,1)S(1)}, bf16[256,32]{0,1:T(8,128)(2,1)}, u32[]{:S(2)}) copy-start(bf16[256,32]{0,1:T(8,128)(2,1)} %param.24) | copy-start | bytes 49156
  82.9 20.4 %copy-start.3 = (bf16[512,256]{1,0:T(8,128)(2,1)}, bf16[512,256]{1,0:T(8,128)(2,1)S(1)}, u32[]{:S(2)}) copy-start(bf16[512,256]{1,0:T(8,128)(2,1)S(1)} %multiply_convert_fusion.normed_ffn_ref) | copy-start | bytes 786436
  83.7 15.7 %copy-start.18 = (s32[512,8]{0,1:T(8,128)S(1)}, s32[512,8]{0,1:T(8,128)}, u32[]{:S(2)}) copy-start(s32[512,8]{0,1:T(8,128)} %param.16) | copy-start | bytes 49156
  83.7 17.5 %copy-start.12 = (bf16[512,256]{1,0:T(8,128)(2,1)S(1)}, bf16[512,256]{1,0:T(8,128)(2,1)}, u32[]{:S(2)}) copy-start(bf16[512,256]{1,0:T(8,128)(2,1)} %cot_ref.1) | copy-start | bytes 786436
  99.6 3.7 %copy-start.10 = (f32[32,512]{1,0:T(8,128)}, f32[32,512]{1,0:T(8,128)S(1)}, u32[]{:S(2)}) copy-start(f32[32,512]{1,0:T(8,128)S(1)} %fusion.42.probs_ref) | copy-start | bytes 196612
  173.7 6.3 %copy-start.19 = (f32[256]{0:T(256)S(1)}, f32[256]{0:T(256)}, u32[]{:S(2)}) copy-start(f32[256]{0:T(256)} %param.18) | copy-start | bytes 3076
  173.7 7.2 %copy-start.5 = (bf16[256,512]{1,0:T(8,128)(2,1)S(1)}, bf16[256,512]{1,0:T(8,128)(2,1)}, u32[]{:S(2)}) copy-start(bf16[256,512]{1,0:T(8,128)(2,1)} %param.19) | copy-start | bytes 786436
  173.7 7.2 %copy-start.8 = (bf16[256,256]{1,0:T(8,128)(2,1)S(1)}, bf16[256,256]{1,0:T(8,128)(2,1)}, u32[]{:S(2)}) copy-start(bf16[256,256]{1,0:T(8,128)(2,1)} %param.21) | copy-start | bytes 393220
  173.7 7.2 %copy-start.9 = (bf16[256,256]{1,0:T(8,128)(2,1)S(1)}, bf16[256,256]{1,0:T(8,128)(2,1)}, u32[]{:S(2)}) copy-start(bf16[256,256]{1,0:T(8,128)(2,1)} %param.20) | copy-start | bytes 393220
  293.1 1.3 copy-start.7
  294.3 1.9 copy-start.13
  294.4 4.2 %copy-start.17 = (f32[16,8,256]{2,1,0:T(8,128)S(1)}, f32[16,8,256]{2,1,0:T(8,128)}, u32[]{:S(2)}) copy-start(f32[16,8,256]{2,1,0:T(8,128)} %get-tuple-element.55) | copy-start | bytes 393220
  294.4 4.8 %copy-start.15 = (bf16[512,256]{1,0:T(8,128)(2,1)S(1)}, bf16[512,256]{1,0:T(8,128)(2,1)}, u32[]{:S(2)}) copy-start(bf16[512,256]{1,0:T(8,128)(2,1)} %get-tuple-element.98) | copy-start | bytes 786436
  294.5 5.4 %copy-start.14 = (bf16[512,256]{1,0:T(8,128)(2,1)S(1)}, bf16[512,256]{1,0:T(8,128)(2,1)}, u32[]{:S(2)}) copy-start(bf16[512,256]{1,0:T(8,128)(2,1)} %get-tuple-element.99) | copy-start | bytes 786436

commit v2 on v1

--- a/solution.py
+++ b/solution.py
@@ -77,171 +77,6 @@
 
 def expert_of(x, z, c):
     return c * 16 + x * 4 + z
-
-
-def exchange(number, *items):
-    modes = [i[0] for i in items]
-    groups = [i[1] for i in items]
-    arrays = [i[2] for i in items]
-    count = len(items)
-    most = max([8] + [size_of(g) for g in groups])
-    moves = {}
-    for g in groups:
-        for move in steps_of(g):
-            full = {d: k for d, k in zip(g, move) if k}
-            moves[tuple(sorted(full.items()))] = (g, move)
-    delivers = "deliver" in modes
-
-    def kernel(*refs):
-        ins, outs = refs[:count], refs[count : 2 * count]
-        send, recv, local = refs[2 * count :]
-        dp, z, c = (lax.axis_index(a) for a in AXES)
-        y_hi, x, core = dp // 8, (dp // 2) % 4, dp % 2
-        barrier = pltpu.get_barrier_semaphore()
-        owner = c * 8 + x * 2 + z // 2
-        slot = (z % 2) * 4 + y_hi * 2 + core
-        for g, move in moves.values():
-            pl.semaphore_signal(
-                barrier, inc=1, device_id=goal(g, move)[1], device_id_type=MESH
-            )
-        sources = []
-        if delivers:
-            for i in range(8):
-                place = {
-                    "dp": ((i // 2) % 2) * 8 + x * 2 + i % 2,
-                    "row": core * 2 + i // 4,
-                    "col": y_hi,
-                }
-                mine = (place["dp"] == dp) & (place["row"] == z) & (place["col"] == c)
-                sources.append((place, mine))
-
-                @pl.when(jnp.logical_not(mine))
-                def _(place=place):
-                    pl.semaphore_signal(
-                        barrier, inc=1, device_id=place, device_id_type=MESH
-                    )
-
-            @pl.when(owner == dp)
-            def _():
-                pl.semaphore_wait(barrier, len(moves) + 7)
-
-            @pl.when(owner != dp)
-            def _():
-                pl.semaphore_wait(barrier, len(moves) + 8)
-
-        else:
-            pl.semaphore_wait(barrier, len(moves))
-
-        def block(a, index, place):
-            if modes[a] == "split":
-                return ins[a].at[index]
-            if modes[a] == "expert":
-                e = expert_of(x, place["row"], place["col"])
-                return ins[a].at[e, pl.ds(pl.multiple_of(core * 128, 128), 128), :]
-            return ins[a]
-
-        copies = []
-        for a in range(count):
-            if modes[a] == "deliver":
-                continue
-            me = member(groups[a])
-            for step, move in enumerate(steps_of(groups[a])):
-                index, place = goal(groups[a], move)
-                copies.append(
-                    pltpu.make_async_remote_copy(
-                        src_ref=block(a, index, place),
-                        dst_ref=outs[a] if modes[a] == "swap" else outs[a].at[me],
-                        send_sem=send.at[a, step],
-                        recv_sem=recv.at[a, step],
-                        device_id=place,
-                        device_id_type=MESH,
-                    )
-                )
-                copies[-1].start()
-        for a in range(count):
-            if modes[a] not in ("swap", "deliver"):
-                me = member(groups[a])
-                source = block(a, me, {"row": z, "col": c})
-                copies.append(pltpu.make_async_copy(source, outs[a].at[me], local.at[a]))
-                copies[-1].start()
-        for a in range(count):
-            if modes[a] == "deliver":
-
-                def remote(j, a=a):
-                    return pltpu.make_async_remote_copy(
-                        src_ref=ins[a].at[j],
-                        dst_ref=outs[a].at[slot],
-                        send_sem=send.at[a, j],
-                        recv_sem=recv.at[a, slot],
-                        device_id={"dp": owner, "row": j % 4, "col": j // 4},
-                        device_id_type=MESH,
-                    )
-
-                def own(j):
-                    return (owner == dp) & (z == j % 4) & (c == j // 4)
-
-                for kz, kc in ((2, 1), (2, 0), (1, 1), (3, 1), (1, 0), (3, 0), (0, 1), (0, 0)):
-                    j = (z + kz) % 4 + 4 * ((c + kc) % 2)
-
-                    @pl.when(own(j))
-                    def _(j=j, a=a):
-                        copy = pltpu.make_async_copy(
-                            ins[a].at[j], outs[a].at[slot], local.at[a]
-                        )
-                        copy.start()
-                        copy.wait()
-
-                    @pl.when(jnp.logical_not(own(j)))
-                    def _(j=j):
-                        remote(j).start()
-
-                for j in range(8):
-
-                    @pl.when(jnp.logical_not(own(j)))
-                    def _(j=j):
-                        remote(j).wait_send()
-
-                for i in range(8):
-
-                    @pl.when(jnp.logical_not(sources[i][1]))
-                    def _(i=i, a=a):
-                        pltpu.make_async_remote_copy(
-                            src_ref=ins[a].at[0],
-                            dst_ref=outs[a].at[i],
-                            send_sem=send.at[a, 0],
-                            recv_sem=recv.at[a, i],
-                            device_id={"dp": owner, "row": 0, "col": 0},
-                            device_id_type=MESH,
-                        ).wait_recv()
-
-        for copy in copies:
-            copy.wait()
-
-    def result(m, g, v):
-        shape = v.shape
-        if m == "share":
-            shape = (size_of(g),) + shape
-        elif m == "expert":
-            shape = (8, 128, 256)
-        return jax.ShapeDtypeStruct(shape, v.dtype)
-
-    spec = pl.BlockSpec(memory_space=pltpu.VMEM)
-    far = pl.BlockSpec(memory_space=pl.ANY)
-    return pl.pallas_call(
-        kernel,
-        out_shape=[result(m, g, v) for m, g, v in items],
-        in_specs=[far if m == "expert" else spec for m in modes],
-        out_specs=[spec] * count,
-        scratch_shapes=[
-            pltpu.SemaphoreType.DMA((count, most)),
-            pltpu.SemaphoreType.DMA((count, most)),
-            pltpu.SemaphoreType.DMA((count,)),
-        ],
-        compiler_params=pltpu.CompilerParams(
-            collective_id=number, has_side_effects=True, vmem_limit_bytes=60 * 1024 * 1024
-        ),
-        name=f"exchange{number}",
-    )(*arrays)
 
 
 def expert_kernel(
@@ -491,16 +326,288 @@
     )(*operands)
 
 
+def as_row(column):
+    return jnp.transpose(jnp.broadcast_to(column, (512, 128)))[:8]
+
+
+def as_column(row):
+    return jnp.transpose(jnp.broadcast_to(row, (8, 512)))[:, :1]
+
+
+def launch(send, recv, used, mode, group, source, target):
+    me = member(group)
+    copies = []
+    for move in steps_of(group):
+        index, place = goal(group, move)
+        copies.append(
+            pltpu.make_async_remote_copy(
+                src_ref=source(index) if mode == "split" else source,
+                dst_ref=target if mode == "swap" else target.at[me],
+                send_sem=send.at[used[0]],
+                recv_sem=recv.at[used[0]],
+                device_id=place,
+                device_id_type=MESH,
+            )
+        )
+        used[0] += 1
+        copies[-1].start()
+    if mode != "swap":
+        target[me] = source(me)[...] if mode == "split" else source[...]
+    return copies
+
+
+HEAD_OUT = (
+    ((8, 512, 128), LOW),
+    ((8, 128, 256), LOW),
+    ((8, 128, 256), LOW),
+    ((8, 128, 256), LOW),
+    ((2, 512, 512), F32),
+    ((512, 128), LOW),
+    ((512, 128), LOW),
+    ((512, 128), LOW),
+    ((512, 1), F32),
+    ((512, 256), LOW),
+    ((512, 256), F32),
+    ((512, 1), F32),
+    ((512, 256), LOW),
+    ((32, 512), F32),
+    ((32, 512), F32),
+    ((16, 1, 512), jnp.int32),
+    ((16, CAP, 256), LOW),
+    ((16, CAP, 256), LOW),
+    ((16, 8, 256), F32),
+)
+HEAD_SCRATCH = (
+    ((4, 512, 256), LOW),
+    ((8, 256), F32),
+    ((4, 8, 256), F32),
+    ((4, 256, 128), LOW),
+    ((4, 256, 128), LOW),
+    ((4, 256, 128), LOW),
+    ((2, 512, 256), LOW),
+    ((8, 512), F32),
+    ((4, 8, 512), F32),
+    ((32, 512), F32),
+    ((4, 32, 512), F32),
+    ((32, 512), jnp.int32),
+)
+
+
+def head_kernel(
+    x_in, gain1, gain2, w_query, w_key, w_value, w_out, router, ids, segment, cot,
+    cos_q, sin_q, cos_kv, sin_kv, w_gate, w_up, w_down,
+    attended_all, near0, near1, near2, weights_ref, attended, queries, kv, scale_attn,
+    normed_own, resid_ref, scale_ffn, normed_ffn, router_gain, probs_ref, own_rank,
+    sent_x, sent_top, sent_p,
+    x_all, gain, gain_all, kv_w, q_all, kv_all, out_all, square, squares, logit, logits,
+    rank_ref, send, recv, local,
+):
+    dp, z, c = (lax.axis_index(a) for a in AXES)
+    x, core = (dp // 2) % 4, dp % 2
+    barrier = pltpu.get_barrier_semaphore()
+    team = steps_of(TEAM)
+    for move in team:
+        pl.semaphore_signal(
+            barrier, inc=1, device_id=goal(TEAM, move)[1], device_id_type=MESH
+        )
+    pl.semaphore_wait(barrier, len(team))
+    used = [0]
+
+    def begin(mode, group, source, target):
+        return launch(send, recv, used, mode, group, source, target)
+
+    def wait(copies):
+        for copy in copies:
+            copy.wait()
+
+    def shards(w, target, k):
+        half = pl.ds(pl.multiple_of(core * 128, 128), 128)
+        me = member(TEAM)
+        copies = []
+        for move in team:
+            place = goal(TEAM, move)[1]
+            copies.append(
+                pltpu.make_async_remote_copy(
+                    src_ref=w.at[expert_of(x, place["row"], place["col"]), half, :],
+                    dst_ref=target.at[me],
+                    send_sem=send.at[used[0]],
+                    recv_sem=recv.at[used[0]],
+                    device_id=place,
+                    device_id_type=MESH,
+                )
+            )
+            used[0] += 1
+        copies.append(
+            pltpu.make_async_copy(
+                w.at[expert_of(x, z, c), half, :], target.at[me], local.at[k]
+            )
+        )
+        for copy in copies:
+            copy.start()
+        return copies
+
+    gain[...] = jnp.broadcast_to(gain1[...], (8, 256))
+    for j in range(4):
+        kv_w[j, :, :64] = w_key[:, j * 64 : j * 64 + 64]
+        kv_w[j, :, 64:] = w_value[:, j * 64 : j * 64 + 64]
+    first = begin("share", (Z,), x_in, x_all)
+    first += begin("share", (Z,), gain, gain_all)
+
+    def columns(j):
+        return w_query.at[:, pl.ds(pl.multiple_of(j * 128, 128), 128)]
+
+    parts = begin("split", (Z,), columns, q_all)
+    parts += begin("split", (Z,), lambda j: kv_w.at[j], kv_all)
+    parts += begin("share", (SIDE,), w_out, out_all)
+    bulk = shards(w_gate, near0, 0)
+
+    experts = lax.broadcasted_iota(jnp.int32, (EXPERTS, LENGTH), 0)
+    hits = ids[0:1] == experts
+    for k in range(1, 8):
+        hits = hits | (ids[k : k + 1] == experts)
+    at_row = lax.broadcasted_iota(jnp.int32, (LENGTH, LENGTH), 0)
+    at_lane = lax.broadcasted_iota(jnp.int32, (LENGTH, LENGTH), 1)
+    earlier = jnp.where(at_row < at_lane, 1.0, 0.0).astype(LOW)
+    marks = jnp.where(hits, 1.0, 0.0)
+    rank = dot(marks.astype(LOW), earlier, ((1,), (0,)))
+    rank_ref[...] = jnp.where(hits, rank, -1.0).astype(jnp.int32)
+    own = pl.ds(pl.multiple_of(c * 16, 16), 16)
+    mine = rank_ref[own, :]
+    for e in range(16):
+        own_rank[e] = mine[e : e + 1]
+
+    def taken_by(e):
+        places = lax.broadcasted_iota(jnp.int32, (CAP, LENGTH), 0)
+        return own_rank[e] == places
+
+    def place_top(e, _):
+        pick = jnp.where(taken_by(e), 1.0, 0.0).astype(LOW)
+        sent_top[e] = dot(pick, cot[...], ((1,), (0,))).astype(LOW)
+        return 0
+
+    lax.fori_loop(0, 16, place_top, 0)
+
+    wait(first)
+    total = jnp.zeros((LENGTH, 1), F32)
+    for j in range(4):
+        block = x_all[j].astype(F32)
+        total = total + jnp.sum(block * block, axis=1, keepdims=True)
+    scale = lax.rsqrt(total / D + EPSILON)
+    scale_attn[...] = scale
+    residual = x_in[...].astype(F32)
+    normed_own[...] = (residual * scale * gain1[...]).astype(LOW)
+    wait(parts)
+    part_q = jnp.zeros((LENGTH, 128), F32)
+    part_kv = jnp.zeros((LENGTH, 128), F32)
+    for j in range(4):
+        normed = (x_all[j].astype(F32) * scale * gain_all[j, :1]).astype(LOW)
+        part_q = part_q + dot(normed, q_all[j], ((1,), (0,)))
+        part_kv = part_kv + dot(normed, kv_all[j], ((1,), (0,)))
+    low_lane = lax.broadcasted_iota(jnp.int32, (LENGTH, 128), 1) % 64 < 32
+
+    def turn(value, cosine, sine_part):
+        other = jnp.where(low_lane, pltpu.roll(value, 96, 1), pltpu.roll(value, 32, 1))
+        return (value * cosine - other * sine_part).astype(LOW)
+
+    queries[...] = turn(part_q, cos_q[...], sin_q[...])
+    kv[...] = turn(part_kv, cos_kv[...], sin_kv[...])
+    keys, values = kv[:, :64], kv[:, 64:]
+    segment_row = segment[...].astype(F32)
+    allowed = (at_lane <= at_row) & (segment_row == as_column(segment_row))
+    for h in range(2):
+        span = slice(h * HEAD_DIM, h * HEAD_DIM + HEAD_DIM)
+        scores = dot(queries[:, span], keys, ((1,), (1,))) * HEAD_DIM ** (-0.5)
+        scores = jnp.where(allowed, scores, MASKED)
+        top = jnp.max(scores, axis=1, keepdims=True)
+        log_total = top + jnp.log(jnp.sum(jnp.exp(scores - top), axis=1, keepdims=True))
+        weights = jnp.exp(scores - log_total)
+        weights_ref[h] = weights
+        attended[:, span] = dot(weights.astype(LOW), values, ((1,), (0,))).astype(LOW)
+    met = begin("share", TEAM, attended, attended_all)
+    bulk += shards(w_up, near1, 1)
+    wait(met)
+    resid = residual
+    for m in range(8):
+        rows_of = out_all[m // 4, (m % 4) * 128 : (m % 4) * 128 + 128]
+        resid = resid + dot(attended_all[m], rows_of, ((1,), (0,)))
+    resid_ref[...] = resid
+    square[...] = as_row(jnp.sum(resid * resid, axis=1, keepdims=True))
+    met = begin("share", (Z,), square, squares)
+    bulk += shards(w_down, near2, 2)
+    router_gain[...] = lax.dot_general(
+        router[...].astype(F32),
+        resid * gain2[...],
+        (((1,), (1,)), ((), ())),
+        precision=lax.Precision.HIGHEST,
+        preferred_element_type=F32,
+    )
+    wait(met)
+    row = (squares[0, :1] + squares[1, :1]) + (squares[2, :1] + squares[3, :1])
+    scale = as_column(lax.rsqrt(row / D + EPSILON))
+    scale_ffn[...] = scale
+    normed_ffn[...] = (resid_ref[...] * scale * gain2[...]).astype(LOW)
+    logit[...] = dot(router[...], normed_ffn[...], ((1,), (1,)))
+    met = begin("share", (Z,), logit, logits)
+    wait(met)
+    sums = (logits[0] + logits[1]) + (logits[2] + logits[3])
+    chosen = jnp.where(hits, sums, MASKED)
+    chosen = jnp.exp(chosen - jnp.max(chosen, axis=0, keepdims=True)) * marks
+    probs_ref[...] = chosen / jnp.sum(chosen, axis=0, keepdims=True)
+
+    def place_x(e, _):
+        taken = taken_by(e)
+        pick = jnp.where(taken, 1.0, 0.0).astype(LOW)
+        sent_x[e] = dot(pick, normed_ffn[...], ((1,), (0,))).astype(LOW)
+        p = probs_ref[pl.ds(c * 16 + e, 1), :]
+        p = jnp.sum(jnp.where(taken, p, 0.0), axis=1, keepdims=True)
+        sent_p[e] = jnp.zeros((8, 256), F32)
+        sent_p[e, :, :CAP] = jnp.transpose(jnp.broadcast_to(p, (CAP, 128)))[:8]
+        return 0
+
+    lax.fori_loop(0, 16, place_x, 0)
+    wait(bulk)
+
+
+def head_step(number, *operands):
+    spec = pl.BlockSpec(memory_space=pltpu.VMEM)
+    far = pl.BlockSpec(memory_space=pl.ANY)
+    return pl.pallas_call(
+        head_kernel,
+        out_shape=[jax.ShapeDtypeStruct(*v) for v in HEAD_OUT],
+        in_specs=[spec] * (len(operands) - 3) + [far] * 3,
+        out_specs=[spec] * len(HEAD_OUT),
+        scratch_shapes=[pltpu.VMEM(*v) for v in HEAD_SCRATCH]
+        + [
+            pltpu.SemaphoreType.DMA((56,)),
+            pltpu.SemaphoreType.DMA((56,)),
+            pltpu.SemaphoreType.DMA((3,)),
+        ],
+        compiler_params=pltpu.CompilerParams(
+            collective_id=number, has_side_effects=True, vmem_limit_bytes=60 * 1024 * 1024
+        ),
+        name="head",
+    )(*operands)
+
+
 TAIL_OUT = (
+    ((2, 256, 256), F32),
+    ((2, 256, 256), F32),
+    ((2, 256, 256), F32),
+    ((256, 512), F32),
+    ((256, 256), F32),
+    ((256, 256), F32),
+    ((512, 256), F32),
+    ((32, 256), F32),
+    ((8, 256), F32),
+    ((512, 256), LOW),
+    ((512, 256), LOW),
+)
+TAIL_SCRATCH = (
     ((8, 3, 128, 256), LOW),
     ((16, 32, 256), LOW),
     ((16, 8, 256), F32),
     ((16, 16, 1024), LOW),
     ((16, 8, 256), F32),
-    ((512, 256), LOW),
-    ((512, 256), LOW),
-)
-TAIL_SCRATCH = (
     ((512, 256), LOW),
     ((2, 16, 512), F32),
     ((8, 8, 512), F32),
@@ -535,26 +642,20 @@
 TAIL_SEMS = 224
 
 
-def as_row(column):
-    return jnp.transpose(jnp.broadcast_to(column, (512, 128)))[:8]
-
-
-def as_column(row):
-    return jnp.transpose(jnp.broadcast_to(row, (8, 512)))[:, :1]
-
-
 def tail_kernel(
     home_ref, gain_own_ref, pull_ref, router_gain_ref, w_out_ref, scaled0_ref, scaled1_ref,
     kept_ref, resid_mid_ref, cot_ref, scale_ffn_ref, gain2_ref, probs_ref, router_ref,
-    normed_ffn_ref, attended_all_ref, attended_ref, queries_ref, keys_ref, values_ref,
-    weights_ref, cos_q_ref, sin_q_ref, cos_kv_ref, sin_kv_ref, whole_ref, normed_own_ref,
-    x_in_ref, scale_attn_ref, gain1_ref, own_rank_ref, owned_ref, out_sum_ref,
-    router_sum_ref, joined_sum_ref, gains_ref, block_out_ref, grad_input_ref, home2_ref,
-    gain_pair_ref, pulls_ref, router_pull_ref, out_heads_ref, back0_ref, back1_ref, mid_ref,
-    mid_all_ref, grad_mid_ref, g_out_ref, out_parts_ref, out_chunk_ref, g_router_ref,
-    router_parts_ref, router_chunk_ref, proj_ref, proj_all_ref, flat_ref, gn_ref, gn2_ref,
-    pull2_ref, pulls2_ref, g_joined_ref, joined_parts_ref, joined_chunk_ref, gains_own_ref,
-    moe_sum_ref, moe_ref, moe2_ref, send, recv,
+    normed_ffn_ref, attended_all_ref, attended_ref, queries_ref, kv_ref, weights_ref,
+    cos_q_ref, sin_q_ref, cos_kv_ref, sin_kv_ref, whole_ref, normed_own_ref, x_in_ref,
+    scale_attn_ref, gain1_ref, own_rank_ref, grad_gate_ref, grad_up_ref, grad_down_ref,
+    grad_query_ref, grad_key_ref, grad_value_ref, grad_out_ref, grad_router_ref,
+    gain_sum_ref, block_out_ref, grad_input_ref, owned_ref, out_sum_ref, router_sum_ref,
+    joined_sum_ref, gains_ref, home2_ref, gain_pair_ref, pulls_ref, router_pull_ref,
+    out_heads_ref, back0_ref, back1_ref, mid_ref, mid_all_ref, grad_mid_ref, g_out_ref,
+    out_parts_ref, out_chunk_ref, g_router_ref, router_parts_ref, router_chunk_ref,
+    proj_ref, proj_all_ref, flat_ref, gn_ref, gn2_ref, pull2_ref, pulls2_ref, g_joined_ref,
+    joined_parts_ref, joined_chunk_ref, gains_own_ref, moe_sum_ref, moe_ref, moe2_ref, send,
+    recv,
 ):
     dp, z, c = (lax.axis_index(a) for a in AXES)
     y_hi, x, core = dp // 8, (dp // 2) % 4, dp % 2
@@ -593,25 +694,7 @@
     used = [0]
 
     def begin(mode, group, source, target):
-        me = member(group)
-        copies = []
-        for move in steps_of(group):
-            index, place = goal(group, move)
-            copies.append(
-                pltpu.make_async_remote_copy(
-                    src_ref=source(index) if mode == "split" else source,
-                    dst_ref=target if mode == "swap" else target.at[me],
-                    send_sem=send.at[used[0]],
-                    recv_sem=recv.at[used[0]],
-                    device_id=place,
-                    device_id_type=MESH,
-                )
-            )
-            used[0] += 1
-            copies[-1].start()
-        if mode != "swap":
-            target[me] = source(me)[...] if mode == "split" else source[...]
-        return copies
+        return launch(send, recv, used, mode, group, source, target)
 
     def wait(copies):
         for copy in copies:
@@ -699,7 +782,7 @@
         grad_att = grad_att + dot(mid_all_ref[j], out_heads_ref[j], ((1,), (1,)))
     grad_att = grad_att.astype(LOW)
     product = grad_att.astype(F32) * attended_ref[...].astype(F32)
-    keys, values = keys_ref[...], values_ref[...]
+    keys, values = kv_ref[:, :64], kv_ref[:, 64:]
     grad_q = []
     grad_k = jnp.zeros((512, HEAD_DIM), F32)
     grad_v = jnp.zeros((512, HEAD_DIM), F32)
@@ -800,6 +883,18 @@
         resid_mid + (moe_ref[...].astype(F32) + moe2_ref[...].astype(F32))
     ).astype(LOW)
     wait(rest)
+    for j in range(16):
+        part = joined_sum_ref[j].astype(F32)
+        at_rows = slice(16 * j, 16 * j + 16)
+        grad_query_ref[at_rows] = part[:, :512]
+        grad_key_ref[at_rows] = part[:, 512:768]
+        grad_value_ref[at_rows] = part[:, 768:]
+        grad_out_ref[32 * j : 32 * j + 32] = out_sum_ref[j].astype(F32)
+        grad_router_ref[2 * j : 2 * j + 2] = router_sum_ref[j, :2]
+    total = gains_ref[0]
+    for j in range(1, 16):
+        total = total + gains_ref[j]
+    gain_sum_ref[...] = total
     for which in range(3):
         for j in range(8):
 
@@ -810,6 +905,13 @@
             @pl.when(jnp.logical_not(sources[j]))
             def _(j=j, which=which):
                 parcel(which, 0, j).wait_recv()
+
+    for which, target in enumerate((grad_gate_ref, grad_up_ref, grad_down_ref)):
+        for i in range(2):
+            for half in range(2):
+                target[i, half * 128 : half * 128 + 128] = owned[i * 4 + half, which].astype(
+                    F32
+                ) + owned[i * 4 + 2 + half, which].astype(F32)
 
 
 def tail_step(number, *operands):
@@ -832,25 +934,11 @@
     half_dim = HEAD_DIM // 2
     exponent = jnp.arange(half_dim).astype(F32) * (2.0 / HEAD_DIM)
     angles = positions.astype(F32)[:, None] * (ROPE_BASE ** (-exponent))[None, :]
-    return (jnp.cos(angles)[:, None, :], jnp.sin(angles)[:, None, :])
-
-
-def rotate(values_in, cosine, sine_part):
-    half_dim = values_in.shape[-1] // 2
-    low_half = values_in[..., :half_dim]
-    high_half = values_in[..., half_dim:]
-    return jnp.concatenate(
-        [low_half * cosine - high_half * sine_part, high_half * cosine + low_half * sine_part],
-        axis=-1,
-    )
+    return (jnp.cos(angles), jnp.sin(angles))
 
 
 def dot(a, b, dims):
     return lax.dot_general(a, b, (dims, ((), ())), preferred_element_type=F32)
-
-
-def rows(vector):
-    return vector.reshape(4, 128)
 
 
 def on_device(
@@ -869,109 +957,77 @@
     w_up,
     w_down,
 ):
-    dp, z, c = (lax.axis_index(a) for a in ("dp", "row", "col"))
-    score_scale = HEAD_DIM ** (-0.5)
-
-    joined = jnp.concatenate(
-        [
-            w_query.reshape(256, 4, 128),
-            w_key.reshape(256, 4, 64),
-            w_value.reshape(256, 4, 64),
-        ],
-        axis=2,
+    cosine, sine_part = rope_tables(jnp.arange(LENGTH, dtype=jnp.int32))
+    idle = jnp.zeros((LENGTH, HEAD_DIM), F32)
+    tables = (
+        jnp.concatenate([cosine] * 4, axis=1),
+        jnp.concatenate([sine_part, -sine_part] * 2, axis=1),
+        jnp.concatenate([cosine, cosine, idle + 1.0], axis=1),
+        jnp.concatenate([sine_part, -sine_part, idle], axis=1),
     )
-    x_all, head_weights, gain_all, out_all = exchange(
+    router = w_router.T
+    gain1, gain2 = norm_gain1.reshape(1, 256), norm_gain2.reshape(1, 256)
+    (
+        attended_all,
+        near_gate,
+        near_up,
+        near_down,
+        weights,
+        attended,
+        queries,
+        kv,
+        scale_attn,
+        normed_own,
+        resid_mid,
+        scale_ffn,
+        normed_ffn,
+        router_gain,
+        probs,
+        own_rank,
+        sent_x,
+        sent_top,
+        sent_p,
+    ) = head_step(
         2,
-        ("share", (Z,), x_in),
-        ("split", (Z,), joined.transpose(1, 0, 2)),
-        ("share", (Z,), norm_gain1.reshape(2, 128)),
-        ("share", (SIDE,), w_out),
+        x_in,
+        gain1,
+        gain2,
+        w_query,
+        w_key,
+        w_value,
+        w_out,
+        router,
+        expert_ids.T,
+        segments,
+        cotangent,
+        *tables,
+        w_gate,
+        w_up,
+        w_down,
     )
-    out_all = out_all.reshape(1024, 256)
-    residual_all = x_all.astype(F32)
-    scale_attn = lax.rsqrt(jnp.sum(residual_all * residual_all, axis=(0, 2)) / D + EPSILON)[
-        :, None
-    ]
-    normed_all = (residual_all * scale_attn[None] * gain_all.reshape(4, 1, 256)).astype(LOW)
-    normed_flat = normed_all.transpose(1, 0, 2).reshape(LENGTH, D)
-    projected = dot(normed_flat, head_weights.reshape(D, 256), ((1,), (0,)))
-    cosine, sine_part = rope_tables(jnp.arange(LENGTH, dtype=jnp.int32))
-    queries = rotate(projected[:, :128].reshape(LENGTH, 2, HEAD_DIM), cosine, sine_part)
-    queries = queries.astype(LOW)
-    keys = rotate(projected[:, 128:192].reshape(LENGTH, 1, HEAD_DIM), cosine, sine_part)
-    keys = keys.astype(LOW)[:, 0]
-    values = projected[:, 192:].astype(LOW)
-    places = jnp.arange(LENGTH, dtype=jnp.int32)
-    segment_row = segments.reshape(-1)
-    allowed = (places[None, :] <= places[:, None]) & (
-        segment_row[None, :] == segment_row[:, None]
+    pulled, gain_rows, scaled0, scaled1, kept = expert_step(
+        7, sent_x, sent_top, sent_p, near_gate, near_up, near_down
     )
-    scores = jnp.einsum("qhd,kd->hqk", queries, keys, preferred_element_type=F32) * score_scale
-    scores = jnp.where(allowed[None], scores, MASKED)
-    top_score = jnp.max(scores, axis=2, keepdims=True)
-    log_total = top_score + jnp.log(jnp.sum(jnp.exp(scores - top_score), axis=2, keepdims=True))
-    weights = jnp.exp(scores - log_total)
-    weights_low = weights.astype(LOW)
-    attended = jnp.einsum("hqk,kd->qhd", weights_low, values, preferred_element_type=F32)
-    attended = attended.astype(LOW).reshape(LENGTH, 128)
-
-    attended_all, near_gate = exchange(
-        4, ("share", TEAM, attended), ("expert", TEAM, w_gate)
-    )
-    attended_flat = attended_all.transpose(1, 0, 2).reshape(LENGTH, 1024)
-    residual = x_in.astype(F32)
-    resid_mid = residual + dot(attended_flat, out_all, ((1,), (0,)))
-    square_parts, near_up = exchange(
-        5,
-        ("share", (Z,), rows(jnp.sum(resid_mid * resid_mid, axis=1))),
-        ("expert", TEAM, w_up),
-    )
-    squares = jnp.sum(square_parts, axis=0).reshape(LENGTH)
-    scale_ffn = lax.rsqrt(squares / D + EPSILON)[:, None]
-    normed_ffn = (resid_mid * scale_ffn * norm_gain2).astype(LOW)
-    router = w_router.T
-    router_gain = lax.dot_general(
-        router.astype(F32),
-        resid_mid * norm_gain2,
-        (((1,), (1,)), ((), ())),
-        precision=lax.Precision.HIGHEST,
-        preferred_element_type=F32,
-    )
-    logit_parts, near_down = exchange(
-        6,
-        ("share", (Z,), dot(router, normed_ffn, ((1,), (1,)))),
-        ("expert", TEAM, w_down),
-    )
-    logits = jnp.sum(logit_parts, axis=0)
-
-    experts = jnp.arange(EXPERTS, dtype=jnp.int32)[:, None]
-    hits = jnp.any(expert_ids.T[None, :, :] == experts[:, :, None], axis=1)
-    chosen = jnp.where(hits, logits, MASKED)
-    chosen = jnp.where(hits, jnp.exp(chosen - jnp.max(chosen, axis=0, keepdims=True)), 0.0)
-    probs = chosen / jnp.sum(chosen, axis=0, keepdims=True)
-    earlier = (places[:, None] < places[None, :]).astype(LOW)
-    rank = dot(hits.astype(LOW), earlier, ((1,), (0,)))
-    rank = jnp.where(hits, rank, -1.0).astype(jnp.int32)
-    own_rank = lax.dynamic_slice(rank, (c * 16, 0), (16, LENGTH))
-    own_probs = lax.dynamic_slice(probs, (c * 16, 0), (16, LENGTH))
-    taken = own_rank[:, None, :] == jnp.arange(CAP, dtype=jnp.int32)[None, :, None]
-    pick = taken.astype(LOW)
-    sent_x = jnp.einsum("est,td->esd", pick, normed_ffn, preferred_element_type=F32)
-    sent_top = jnp.einsum("est,td->esd", pick, cotangent, preferred_element_type=F32)
-    slot_probs = jnp.sum(jnp.where(taken, own_probs[:, None, :], 0.0), axis=2)
-    slot_probs = jnp.pad(slot_probs, ((0, 0), (0, 96)))
-    slot_probs = jnp.broadcast_to(slot_probs[:, None, :], (16, 8, 256))
-    pulled, gain_rows, scaled0, scaled1, kept = expert_step(
-        7, sent_x.astype(LOW), sent_top.astype(LOW), slot_probs, near_gate, near_up, near_down
-    )
-
-    home = jnp.einsum("est,esd->td", pick, pulled, preferred_element_type=F32).astype(LOW)
+
+    taken = own_rank == jnp.arange(CAP, dtype=jnp.int32)[None, :, None]
+    home = jnp.einsum("est,esd->td", taken.astype(LOW), pulled, preferred_element_type=F32)
+    home = home.astype(LOW)
     gain_rows = gain_rows[:, 0, :CAP]
     own_gain = jnp.sum(jnp.where(taken, gain_rows[:, :, None], 0.0), axis=1)
     pull = jnp.sum(home.astype(F32) * norm_gain2 * resid_mid, axis=1)
-    cos_part, sin_part = cosine[:, 0], sine_part[:, 0]
-    idle = jnp.zeros((LENGTH, HEAD_DIM), F32)
-    owned, out_sum, router_sum, joined_sum, gains, block_out, grad_input = tail_step(
+    (
+        grad_gate,
+        grad_up,
+        grad_down,
+        grad_query,
+        grad_key,
+        grad_value,
+        grad_out,
+        grad_router,
+        gain_sum,
+        block_out,
+        grad_input,
+    ) = tail_step(
         11,
         home,
         own_gain,
@@ -984,42 +1040,34 @@
         resid_mid,
         cotangent,
         scale_ffn,
-        norm_gain2.reshape(1, 256),
+        gain2,
         probs,
         router,
         normed_ffn,
         attended_all,
         attended,
-        queries.reshape(LENGTH, 128),
-        keys,
-        values,
+        queries,
+        kv,
         weights,
-        jnp.concatenate([cos_part] * 4, axis=1),
-        jnp.concatenate([sin_part, -sin_part] * 2, axis=1),
-        jnp.concatenate([cos_part, cos_part, idle + 1.0], axis=1),
-        jnp.concatenate([sin_part, -sin_part, idle], axis=1),
+        *tables,
         jnp.concatenate([w_query, w_key, w_value], axis=1),
-        (residual * scale_attn * norm_gain1).astype(LOW),
+        normed_own,
         x_in,
         scale_attn,
-        norm_gain1.reshape(1, 256),
-        own_rank.reshape(16, 1, LENGTH),
+        gain1,
+        own_rank,
     )
-    joined_sum = joined_sum.reshape(256, 1024).astype(F32)
-    gain_sum = jnp.sum(gains, axis=0)
-    owned = jnp.sum(owned.astype(F32).reshape(2, 2, 2, 3, 128, 256), axis=1)
-    owned = owned.transpose(2, 0, 1, 3, 4).reshape(3, 2, 256, 256)
     return (
         block_out,
         grad_input,
-        joined_sum[:, :512],
-        joined_sum[:, 512:768],
-        joined_sum[:, 768:],
-        out_sum.reshape(512, 256).astype(F32),
-        router_sum[:, :2].reshape(EXPERTS, 256).T,
-        owned[0],
-        owned[1],
-        owned[2],
+        grad_query,
+        grad_key,
+        grad_value,
+        grad_out,
+        grad_router.T,
+        grad_gate,
+        grad_up,
+        grad_down,
         gain_sum[0],
         gain_sum[1],
     )

time: 301 us -> 265 us (0.88)
  other arithmetic: 17.2 us -> 5.43 us
  matrix products: 14 us -> 3.65 us
  Pallas kernels: 248 us -> 241 us
  local copies, waits for them, and re-layouts: 20.1 us -> 13.6 us
    dot_general x10 -> x1, matrix products: 14 us -> 3.65 us  [on_device(): jnp.einsum('est,esd->td', taken.astype(LOW), pulled, preferred_element_ty...]
    pallas_call x4 -> x1, Pallas kernels: 77 us -> 68.1 us  [head_step(): pl.pallas_call(head_kernel, out_shape=[jax.ShapeDtypeStruct(*v) for v in...]
    reduce_sum x8 -> x0, other arithmetic: 6.58 us -> none  [the longest x1 1.88 us: on_device(): owned = jnp.sum(owned.astype(F32).reshape(2, 2, 2, 3, 128, 256), axis=1)]
    unnamed x55 -> x38, local copies, waits for them, and re-layouts: 5.59 us -> 10.6 us
    slice x7 -> x0, local copies, waits for them, and re-layouts: 4.84 us -> none  [the longest x1 1.18 us: on_device(): owned[2]]
where the time goes in v2:
time: 265 us; the launch traced here: 264 us
  Pallas kernels  241 us (91%)
  local copies, waits for them, and re-layouts  13.6 us (5%)
  other arithmetic  5.43 us (2%)
  matrix products  3.65 us (1%)
    pallas_call x1, Pallas kernels, tail_step(): pl.pallas_call(tail_kernel, out_shape=[jax.ShapeDtypeStruct(*v) for v in...  109 us
    pallas_call x1, Pallas kernels, head_step(): pl.pallas_call(head_kernel, out_shape=[jax.ShapeDtypeStruct(*v) for v in...  68.1 us
    pallas_call x1, Pallas kernels, expert_step(): pl.pallas_call(expert_kernel, out_shape=[rows_of, jax.ShapeDtypeStruct((1...  63.1 us
    unnamed x38, local copies, waits for them, and re-layouts  10.6 us

profile of v2, /device:TPU:1, one launch (start us, length us, event | category | flops | bytes accessed | tf_op | source)
XLA Modules:
  0.0 264.2 jit_solution(11403326618328993431)
XLA Ops:
  0.7 1.0 multiply_sine_fusion
  1.7 0.1 pad.5.clone
  1.8 0.1 pad.8.clone
  1.8 1.4 fusion.4
  3.2 68.1 %head.1 = (bf16[8,512,128]{2,1,0:T(8,128)(2,1)}, bf16[8,128,256]{2,1,0:T(8,128)(2,1)}, bf16[8,128,256]{2,1,0:T(8,128)(2,1)}, bf16[8,128,256]{2,1,0:T(8,128)(2,1)...) custom-call(bf16[512,256]{1,0:T(8,128)(2,1)} %x_in_ref.1, ...), custom_call_target="tpu_custom_call" | custom-call | tf_op jit(solution)/shard_map/head/pallas_call | solution.py:574
  71.3 0.0 copy-start.10
  71.3 0.0 copy-start.3
  71.3 0.0 copy-start.12
  71.4 63.1 %expert.1 = (bf16[16,160,256]{2,1,0:T(8,128)(2,1)}, f32[16,8,256]{2,1,0:T(8,128)}, bf16[16,80,256]{2,1,0:T(8,128)(2,1)}, bf16[16,80,256]{2,1,0:T(8,128)(2,1)}, bf16[8,3,128,256]{3,2,1,0:T(8,128)(2,1)}) custom-call(bf16[16,160,256]{2,1,0:T(8,128)(2,1)} %get-tuple-element.48.sent_x, bf16[16,160,256]{2,1,0:T(8,128)(2,1)} %get-tuple-element.49.sent_top, ...), custom_call_target="tpu_custom_call" | custom-call | tf_op jit(solution)/shard_map/expert/pallas_call | solution.py:279
  134.5 0.9 slice.9
  135.4 0.0 copy-done.10
  135.5 2.2 select_reduce_fusion.gain_own_ref
  137.6 0.0 copy-done.3
  137.6 0.0 copy-start.2
  137.7 3.7 %multiply_reduce_fusion = (f32[512]{0:T(512)S(1)}, bf16[512,256]{1,0:T(8,128)(2,1)}) fusion(f32[512,256]{1,0:T(8,128)S(1)} %copy-done.3, f32[256]{0:T(256)S(1)} %copy-done.12, bf16[16,160,256]{2,1,0:T(8,128)(2,1)} %get-tuple-element.54, s32[16,512]{1,0:T(8,128)S(1)} %bitcast.21), kind=kOutput, calls=%fused_computation.7 | convolution fusion | flops 673054208 | bytes 2132992 | tf_op jit(solution)/shard_map/est,esd->td/dot_general | solution.py:1013
  141.3 0.6 broadcast_in_dim.31.pull_ref
  141.9 0.0 copy-done.1
  141.9 0.9 pad_maximum_fusion.whole_ref
  142.8 109.4 %tail.1 = (f32[2,256,256]{2,1,0:T(8,128)}, f32[2,256,256]{2,1,0:T(8,128)}, f32[2,256,256]{2,1,0:T(8,128)}, f32[256,512]{1,0:T(8,128)}, f32[256,256]{1,0:T(8,128)...) custom-call(bf16[512,256]{1,0:T(8,128)(2,1)} %get-tuple-element.92.h, ...), custom_call_target="tpu_custom_call" | custom-call | tf_op jit(solution)/shard_map/tail/pallas_call | solution.py:919
  252.3 1.4 fusion.7
  253.6 1.7 copy.45
  255.4 1.7 copy.46
  257.0 1.9 copy.47
  259.0 0.7 copy.48
  259.7 0.0 copy-done.8
  259.7 0.7 copy.49
  260.4 0.8 copy.50
  261.2 0.6 copy.51
  261.8 0.0 copy-done.6
  261.8 0.8 copy.52
  262.6 0.8 copy.53
  263.4 0.8 copy.54
  (23 shorter events, 0.1 us)
Async XLA Ops:
  71.3 64.1 %copy-start.10 = (s32[16,1,512]{2,1,0:T(1,128)S(1)}, s32[16,1,512]{2,1,0:T(1,128)}, u32[]{:S(2)}) copy-start(s32[16,1,512]{2,1,0:T(1,128)} %get-tuple-element.47.own_rank_ref) | copy-start | bytes 98308
  71.3 66.3 %copy-start.3 = (f32[512,256]{1,0:T(8,128)S(1)}, f32[512,256]{1,0:T(8,128)}, u32[]{:S(2)}) copy-start(f32[512,256]{1,0:T(8,128)} %get-tuple-element.56.resid_mid_ref) | copy-start | bytes 1572868
  71.3 66.3 %copy-start.12 = (f32[256]{0:T(256)S(1)}, f32[256]{0:T(256)}, u32[]{:S(2)}) copy-start(f32[256]{0:T(256)} %param.23) | copy-start | bytes 3076
  137.6 4.3 %copy-start = (bf16[256,512]{1,0:T(8,128)(2,1)S(1)}, bf16[256,512]{1,0:T(8,128)(2,1)}, u32[]{:S(2)}) copy-start(bf16[256,512]{1,0:T(8,128)(2,1)} %w_query.1) | copy-start | bytes 786436
  137.6 4.3 %copy-start.1 = (bf16[256,256]{1,0:T(8,128)(2,1)S(1)}, bf16[256,256]{1,0:T(8,128)(2,1)}, u32[]{:S(2)}) copy-start(bf16[256,256]{1,0:T(8,128)(2,1)} %w_key.1) | copy-start | bytes 393220
  137.6 4.3 %copy-start.2 = (bf16[256,256]{1,0:T(8,128)(2,1)S(1)}, bf16[256,256]{1,0:T(8,128)(2,1)}, u32[]{:S(2)}) copy-start(bf16[256,256]{1,0:T(8,128)(2,1)} %w_value.1) | copy-start | bytes 393220
  252.2 6.7 %copy-start.9 = (f32[256,256]{1,0:T(8,128)S(1)}, f32[256,256]{1,0:T(8,128)}, u32[]{:S(2)}) copy-start(f32[256,256]{1,0:T(8,128)} %get-tuple-element.110) | copy-start | bytes 786436
  252.2 7.4 %copy-start.8 = (f32[256,256]{1,0:T(8,128)S(1)}, f32[256,256]{1,0:T(8,128)}, u32[]{:S(2)}) copy-start(f32[256,256]{1,0:T(8,128)} %get-tuple-element.111) | copy-start | bytes 786436
  252.2 8.1 %copy-start.7 = (f32[512,256]{1,0:T(8,128)S(1)}, f32[512,256]{1,0:T(8,128)}, u32[]{:S(2)}) copy-start(f32[512,256]{1,0:T(8,128)} %get-tuple-element.112) | copy-start | bytes 1572868
  253.6 7.5 %copy-start.11 = (f32[32,256]{1,0:T(8,128)S(1)}, f32[32,256]{1,0:T(8,128)}, u32[]{:S(2)}) copy-start(f32[32,256]{1,0:T(8,128)} %get-tuple-element.77) | copy-start | bytes 98308
  253.6 8.2 %copy-start.6 = (f32[2,256,256]{2,1,0:T(8,128)S(1)}, f32[2,256,256]{2,1,0:T(8,128)}, u32[]{:S(2)}) copy-start(f32[2,256,256]{2,1,0:T(8,128)} %get-tuple-element.114) | copy-start | bytes 1572868
  257.0 5.6 %copy-start.5 = (f32[2,256,256]{2,1,0:T(8,128)S(1)}, f32[2,256,256]{2,1,0:T(8,128)}, u32[]{:S(2)}) copy-start(f32[2,256,256]{2,1,0:T(8,128)} %get-tuple-element.115) | copy-start | bytes 1572868
  259.0 4.4 %copy-start.4 = (f32[2,256,256]{2,1,0:T(8,128)S(1)}, f32[2,256,256]{2,1,0:T(8,128)}, u32[]{:S(2)}) copy-start(f32[2,256,256]{2,1,0:T(8,128)} %get-tuple-element.116) | copy-start | bytes 1572868

commit v3 on v2

--- a/solution.py
+++ b/solution.py
@@ -80,8 +80,9 @@
 
 
 def expert_kernel(
-    sent_x, sent_top, sent_p, near0, near1, near2,
-    returned, gains_back, scaled0, scaled1, total,
+    sent_x, sent_top, sent_p, own_rank, near0, near1, near2,
+    home, own_gain, scaled0, scaled1, total,
+    returned, gains_back, home_sum,
     slots_x, slots_top, slots_p, far0, far1, far2, pulled, gains,
     gate_w, up_w, down_w, rows_in, rows_top, hidden_s, gate_s, up_s, out_s, gate_g, up_g,
     block_s, kept, given, other,
@@ -256,38 +257,60 @@
         return 0
 
     lax.fori_loop(0, 8, add, 0)
-    for move in steps:
-        index, place = goal(PLANE, move)
-        for k, (source, target) in enumerate(
-            ((pulled.at[0, 0], returned), (gains.at[0], gains_back))
-        ):
-            copy = pltpu.make_async_remote_copy(
-                src_ref=source,
-                dst_ref=target.at[index],
-                send_sem=send_back.at[k, index],
-                recv_sem=recv_back.at[k, index],
-                device_id=place,
-                device_id_type=MESH,
-            )
-            copy.wait_send()
-            copy.wait_recv()
+    home_sum[...] = jnp.zeros((LENGTH, 256), F32)
+
+    def collect(n, _):
+        sx = (x + 6 - n // 4) % 4
+        sz = (z + 4 - (2 + 3 * (n % 4)) % 4) % 4
+        index = 4 * sx + sz
+
+        @pl.when(index != me)
+        def _():
+            for copy in go_back(sx, sz, pulled.at[0, 0], gains.at[0]):
+                copy.wait_send()
+            for k, (source, target) in enumerate(
+                ((pulled.at[0, 0], returned), (gains.at[0], gains_back))
+            ):
+                pltpu.make_async_remote_copy(
+                    src_ref=source,
+                    dst_ref=target.at[index],
+                    send_sem=send_back.at[k, index],
+                    recv_sem=recv_back.at[k, index],
+                    device_id=home_of(sx, sz)[0],
+                    device_id_type=MESH,
+                ).wait_recv()
+
+        places = lax.broadcasted_iota(jnp.int32, (CAP, LENGTH), 0)
+        taken = own_rank[index] == places
+        pick = jnp.where(taken, 1.0, 0.0).astype(LOW)
+        home_sum[...] += dot(pick, returned[index], ((0,), (0,)))
+        gain = jnp.transpose(gains_back[index])[:CAP, :1]
+        own_gain[pl.ds(index, 1), :] = jnp.sum(
+            jnp.where(taken, gain, 0.0), axis=0, keepdims=True
+        )
+        return 0
+
+    lax.fori_loop(0, 16, collect, 0)
+    home[...] = home_sum[...].astype(LOW)
 
 
 def expert_step(number, *operands):
     spec = pl.BlockSpec(memory_space=pltpu.VMEM)
-    rows_of = jax.ShapeDtypeStruct((16, CAP, 256), LOW)
     return pl.pallas_call(
         expert_kernel,
         out_shape=[
-            rows_of,
-            jax.ShapeDtypeStruct((16, 8, 256), F32),
+            jax.ShapeDtypeStruct((LENGTH, 256), LOW),
+            jax.ShapeDtypeStruct((16, LENGTH), F32),
             jax.ShapeDtypeStruct((16, CAP // 2, 256), LOW),
             jax.ShapeDtypeStruct((16, CAP // 2, 256), LOW),
             jax.ShapeDtypeStruct((8, 3, 128, 256), LOW),
         ],
-        in_specs=[spec] * 6,
+        in_specs=[spec] * 7,
         out_specs=[spec] * 5,
         scratch_shapes=[
+            pltpu.VMEM((16, CAP, 256), LOW),
+            pltpu.VMEM((16, 8, 256), F32),
+            pltpu.VMEM((LENGTH, 256), F32),
             pltpu.VMEM((16, CAP, 256), LOW),
             pltpu.VMEM((16, CAP, 256), LOW),
             pltpu.VMEM((16, 8, 256), F32),
@@ -590,24 +613,16 @@
 
 
 TAIL_OUT = (
-    ((2, 256, 256), F32),
-    ((2, 256, 256), F32),
-    ((2, 256, 256), F32),
-    ((256, 512), F32),
-    ((256, 256), F32),
-    ((256, 256), F32),
-    ((512, 256), F32),
-    ((32, 256), F32),
-    ((8, 256), F32),
-    ((512, 256), LOW),
-    ((512, 256), LOW),
-)
-TAIL_SCRATCH = (
     ((8, 3, 128, 256), LOW),
     ((16, 32, 256), LOW),
     ((16, 8, 256), F32),
     ((16, 16, 1024), LOW),
     ((16, 8, 256), F32),
+    ((512, 256), LOW),
+    ((512, 256), LOW),
+)
+TAIL_SCRATCH = (
+    ((8, 512), F32),
     ((512, 256), LOW),
     ((2, 16, 512), F32),
     ((8, 8, 512), F32),
@@ -643,19 +658,17 @@
 
 
 def tail_kernel(
-    home_ref, gain_own_ref, pull_ref, router_gain_ref, w_out_ref, scaled0_ref, scaled1_ref,
-    kept_ref, resid_mid_ref, cot_ref, scale_ffn_ref, gain2_ref, probs_ref, router_ref,
-    normed_ffn_ref, attended_all_ref, attended_ref, queries_ref, kv_ref, weights_ref,
-    cos_q_ref, sin_q_ref, cos_kv_ref, sin_kv_ref, whole_ref, normed_own_ref, x_in_ref,
-    scale_attn_ref, gain1_ref, own_rank_ref, grad_gate_ref, grad_up_ref, grad_down_ref,
-    grad_query_ref, grad_key_ref, grad_value_ref, grad_out_ref, grad_router_ref,
-    gain_sum_ref, block_out_ref, grad_input_ref, owned_ref, out_sum_ref, router_sum_ref,
-    joined_sum_ref, gains_ref, home2_ref, gain_pair_ref, pulls_ref, router_pull_ref,
-    out_heads_ref, back0_ref, back1_ref, mid_ref, mid_all_ref, grad_mid_ref, g_out_ref,
-    out_parts_ref, out_chunk_ref, g_router_ref, router_parts_ref, router_chunk_ref,
-    proj_ref, proj_all_ref, flat_ref, gn_ref, gn2_ref, pull2_ref, pulls2_ref, g_joined_ref,
-    joined_parts_ref, joined_chunk_ref, gains_own_ref, moe_sum_ref, moe_ref, moe2_ref, send,
-    recv,
+    home_ref, gain_own_ref, router_gain_ref, w_out_ref, scaled0_ref, scaled1_ref, kept_ref,
+    resid_mid_ref, cot_ref, scale_ffn_ref, gain2_ref, probs_ref, router_ref, normed_ffn_ref,
+    attended_all_ref, attended_ref, queries_ref, kv_ref, weights_ref, cos_q_ref, sin_q_ref,
+    cos_kv_ref, sin_kv_ref, whole_ref, normed_own_ref, x_in_ref, scale_attn_ref, gain1_ref,
+    own_rank_ref, owned_ref, out_sum_ref, router_sum_ref, joined_sum_ref, gains_ref,
+    block_out_ref, grad_input_ref, pull_ref, home2_ref, gain_pair_ref, pulls_ref,
+    router_pull_ref, out_heads_ref, back0_ref, back1_ref, mid_ref, mid_all_ref,
+    grad_mid_ref, g_out_ref, out_parts_ref, out_chunk_ref, g_router_ref, router_parts_ref,
+    router_chunk_ref, proj_ref, proj_all_ref, flat_ref, gn_ref, gn2_ref, pull2_ref,
+    pulls2_ref, g_joined_ref, joined_parts_ref, joined_chunk_ref, gains_own_ref,
+    moe_sum_ref, moe_ref, moe2_ref, send, recv,
 ):
     dp, z, c = (lax.axis_index(a) for a in AXES)
     y_hi, x, core = dp // 8, (dp // 2) % 4, dp % 2
@@ -730,10 +743,15 @@
 
     first = begin("swap", (SIDE,), home_ref, home2_ref)
     first += begin("share", (SIDE,), gain_own_ref, gain_pair_ref)
+    first += begin("share", (Z,), router_gain_ref, router_pull_ref)
+    pull = jnp.sum(
+        home_ref[...].astype(F32) * gain2_ref[...] * resid_mid_ref[...], axis=1, keepdims=True
+    )
+    pull_ref[...] = as_row(pull)
     first += begin("share", TEAM, pull_ref, pulls_ref)
-    first += begin("share", (Z,), router_gain_ref, router_pull_ref)
     heads = begin("split", (Z,), lambda j: w_out_ref.at[j], out_heads_ref)
     back0 = begin("split", PLANE, lambda j: scaled0_ref.at[j], back0_ref)
+    deliver(0)
     wait(first)
     home = home_ref[...].astype(F32) + home2_ref[...].astype(F32)
     grad_prob = jnp.concatenate([gain_pair_ref[0], gain_pair_ref[1]], axis=0)
@@ -773,7 +791,7 @@
         out_parts_ref,
     )
     sums += begin("split", ALL_DP, lambda j: g_router_ref.at[j], router_parts_ref)
-    deliver(0)
+    deliver(1)
 
     wait(heads)
     wait(middle)
@@ -853,7 +871,7 @@
         lambda j: g_joined_ref.at[pl.ds(pl.multiple_of(j * 16, 16), 16)],
         joined_parts_ref,
     )
-    deliver(1)
+    deliver(2)
     wait(back1)
     add_half(back1_ref, 80)
     moe_ref[...] = moe_sum_ref[...].astype(LOW)
@@ -877,24 +895,11 @@
     joined_chunk_ref[...] = total.astype(LOW)
     rest += begin("share", ALL_DP, joined_chunk_ref, joined_sum_ref)
     rest += begin("share", ALL_DP, gains_own_ref, gains_ref)
-    deliver(2)
     wait(moe)
     block_out_ref[...] = (
         resid_mid + (moe_ref[...].astype(F32) + moe2_ref[...].astype(F32))
     ).astype(LOW)
     wait(rest)
-    for j in range(16):
-        part = joined_sum_ref[j].astype(F32)
-        at_rows = slice(16 * j, 16 * j + 16)
-        grad_query_ref[at_rows] = part[:, :512]
-        grad_key_ref[at_rows] = part[:, 512:768]
-        grad_value_ref[at_rows] = part[:, 768:]
-        grad_out_ref[32 * j : 32 * j + 32] = out_sum_ref[j].astype(F32)
-        grad_router_ref[2 * j : 2 * j + 2] = router_sum_ref[j, :2]
-    total = gains_ref[0]
-    for j in range(1, 16):
-        total = total + gains_ref[j]
-    gain_sum_ref[...] = total
     for which in range(3):
         for j in range(8):
 
@@ -906,12 +911,49 @@
             def _(j=j, which=which):
                 parcel(which, 0, j).wait_recv()
 
-    for which, target in enumerate((grad_gate_ref, grad_up_ref, grad_down_ref)):
+
+def finish_kernel(
+    owned, out_sum, router_sum, joined_sum, gains, block_in, grad_in,
+    grad_gate, grad_up, grad_down, grad_query, grad_key, grad_value, grad_out, grad_router,
+    gain_sum, block_out, grad_input,
+):
+    block_out[...] = block_in[...]
+    grad_input[...] = grad_in[...]
+    for j in range(16):
+        part = joined_sum[j].astype(F32)
+        at_rows = slice(16 * j, 16 * j + 16)
+        grad_query[at_rows] = part[:, :512]
+        grad_key[at_rows] = part[:, 512:768]
+        grad_value[at_rows] = part[:, 768:]
+        grad_out[32 * j : 32 * j + 32] = out_sum[j].astype(F32)
+        grad_router[2 * j : 2 * j + 2] = router_sum[j, :2]
+    total = gains[0]
+    for j in range(1, 16):
+        total = total + gains[j]
+    gain_sum[...] = total
+    for which, target in enumerate((grad_gate, grad_up, grad_down)):
         for i in range(2):
             for half in range(2):
                 target[i, half * 128 : half * 128 + 128] = owned[i * 4 + half, which].astype(
                     F32
                 ) + owned[i * 4 + 2 + half, which].astype(F32)
+
+
+def finish_step(*operands):
+    spec = pl.BlockSpec(memory_space=pltpu.VMEM)
+    shapes = (
+        [((2, 256, 256), F32)] * 3
+        + [((256, 512), F32), ((256, 256), F32), ((256, 256), F32), ((512, 256), F32)]
+        + [((32, 256), F32), ((8, 256), F32), ((512, 256), LOW), ((512, 256), LOW)]
+    )
+    return pl.pallas_call(
+        finish_kernel,
+        out_shape=[jax.ShapeDtypeStruct(*v) for v in shapes],
+        in_specs=[spec] * 7,
+        out_specs=[spec] * 11,
+        compiler_params=pltpu.CompilerParams(vmem_limit_bytes=40 * 1024 * 1024),
+        name="finish",
+    )(*operands)
 
 
 def tail_step(number, *operands):
@@ -1005,16 +1047,10 @@
         w_up,
         w_down,
     )
-    pulled, gain_rows, scaled0, scaled1, kept = expert_step(
-        7, sent_x, sent_top, sent_p, near_gate, near_up, near_down
-    )
-
-    taken = own_rank == jnp.arange(CAP, dtype=jnp.int32)[None, :, None]
-    home = jnp.einsum("est,esd->td", taken.astype(LOW), pulled, preferred_element_type=F32)
-    home = home.astype(LOW)
-    gain_rows = gain_rows[:, 0, :CAP]
-    own_gain = jnp.sum(jnp.where(taken, gain_rows[:, :, None], 0.0), axis=1)
-    pull = jnp.sum(home.astype(F32) * norm_gain2 * resid_mid, axis=1)
+    home, own_gain, scaled0, scaled1, kept = expert_step(
+        7, sent_x, sent_top, sent_p, own_rank, near_gate, near_up, near_down
+    )
+
     (
         grad_gate,
         grad_up,
@@ -1027,11 +1063,10 @@
         gain_sum,
         block_out,
         grad_input,
-    ) = tail_step(
+    ) = finish_step(*tail_step(
         11,
         home,
         own_gain,
-        jnp.broadcast_to(pull[None], (8, LENGTH)),
         router_gain,
         w_out.reshape(4, 128, 256),
         scaled0,
@@ -1056,7 +1091,7 @@
         scale_attn,
         gain1,
         own_rank,
-    )
+    ))
     return (
         block_out,
         grad_input,

time: 265 us -> 257 us (0.970)
  local copies, waits for them, and re-layouts: 13.6 us -> 7.84 us
  Pallas kernels: 241 us -> 245 us
  matrix products: 3.65 us -> 0 us
    dot_general x1 -> x0, matrix products: 3.65 us -> none  [on_device(): jnp.einsum('est,esd->td', taken.astype(LOW), pulled, preferred_element_ty...]
    unnamed x38 -> x20, local copies, waits for them, and re-layouts: 10.6 us -> 7.12 us
    pallas_call x1 -> x2, Pallas kernels: 63.1 us -> 65.6 us  [the longest x1 63.6 us: expert_step(): pl.pallas_call(expert_kernel, out_shape=[jax.ShapeDtypeStruct((LENGTH, 25...]
where the time goes in v3:
time: 257 us
  Pallas kernels  245 us (95%)
  local copies, waits for them, and re-layouts  7.84 us (3%)
  other arithmetic  3.27 us (1%)
    pallas_call x1, Pallas kernels, tail_step(): pl.pallas_call(tail_kernel, out_shape=[jax.ShapeDtypeStruct(*v) for v in...  111 us
    pallas_call x1, Pallas kernels, head_step(): pl.pallas_call(head_kernel, out_shape=[jax.ShapeDtypeStruct(*v) for v in...  68.3 us
    pallas_call x1, Pallas kernels, expert_step(): pl.pallas_call(expert_kernel, out_shape=[jax.ShapeDtypeStruct((LENGTH, 25...  63.6 us
    unnamed x20, local copies, waits for them, and re-layouts  7.12 us

profile of v3, /device:TPU:1, one launch (start us, length us, event | category | flops | bytes accessed | tf_op | source)
XLA Modules:
  0.0 256.9 jit_solution(13520709919924799271)
XLA Ops:
  0.7 1.0 multiply_sine_fusion
  1.7 0.1 pad.5.clone
  1.8 0.1 pad.8.clone
  1.8 1.4 fusion
  3.2 68.3 %head.1 = (bf16[8,512,128]{2,1,0:T(8,128)(2,1)}, bf16[8,128,256]{2,1,0:T(8,128)(2,1)}, bf16[8,128,256]{2,1,0:T(8,128)(2,1)}, bf16[8,128,256]{2,1,0:T(8,128)(2,1)...) custom-call(bf16[512,256]{1,0:T(8,128)(2,1)} %x_in_ref.1, ...), custom_call_target="tpu_custom_call" | custom-call | tf_op jit(solution)/shard_map/head/pallas_call | solution.py:597
  71.5 0.0 copy-start.7
  71.5 0.0 copy-start.8
  71.5 0.0 copy-start.9
  71.5 63.6 %expert.1 = (bf16[512,256]{1,0:T(8,128)(2,1)}, f32[16,512]{1,0:T(8,128)}, bf16[16,80,256]{2,1,0:T(8,128)(2,1)}, bf16[16,80,256]{2,1,0:T(8,128)(2,1)}, bf16[8,3,128,256]{3,2,1,0:T(8,128)(2,1)}) custom-call(bf16[16,160,256]{2,1,0:T(8,128)(2,1)} %get-tuple-element.54.sent_x, bf16[16,160,256]{2,1,0:T(8,128)(2,1)} %get-tuple-element.55.sent_top, ...), custom_call_target="tpu_custom_call" | custom-call | tf_op jit(solution)/shard_map/expert/pallas_call | solution.py:299
  135.1 0.0 copy-done.7
  135.2 0.0 copy-done.8
  135.2 0.0 copy-done.9
  135.2 0.9 pad_maximum_fusion.whole_ref
  136.0 111.2 %tail.1 = (bf16[8,3,128,256]{3,2,1,0:T(8,128)(2,1)}, bf16[16,32,256]{2,1,0:T(8,128)(2,1)}, f32[16,8,256]{2,1,0:T(8,128)}, bf16[16,16,1024]{2,1,0:T(8,128)(2,1)},...) custom-call(bf16[512,256]{1,0:T(8,128)(2,1)} %get-tuple-element.61.home_ref, ...), custom_call_target="tpu_custom_call" | custom-call | tf_op jit(solution)/shard_map/tail/pallas_call | solution.py:961
  247.2 0.0 copy-start
  247.2 1.4 copy-done
  248.6 0.0 copy-start.1
  248.6 1.0 copy-done.1
  249.7 0.0 copy-start.2
  249.7 0.9 copy-done.2
  250.6 0.0 copy-start.3
  250.6 0.9 copy-done.3
  251.6 0.0 copy-start.4
  251.6 0.9 copy-done.4
  252.5 0.0 copy-start.5
  252.5 0.9 copy-done.5
  253.4 0.0 copy-start.6
  253.4 0.9 copy-done.6
  254.3 2.0 finish.1
  256.4 0.6 fusion.3
  (4 shorter events, 0.0 us)
Async XLA Ops:
  71.5 63.6 %copy-start.7 = (bf16[256,512]{1,0:T(8,128)(2,1)S(1)}, bf16[256,512]{1,0:T(8,128)(2,1)}, u32[]{:S(2)}) copy-start(bf16[256,512]{1,0:T(8,128)(2,1)} %w_query.1) | copy-start | bytes 786436
  71.5 63.6 %copy-start.8 = (bf16[256,256]{1,0:T(8,128)(2,1)S(1)}, bf16[256,256]{1,0:T(8,128)(2,1)}, u32[]{:S(2)}) copy-start(bf16[256,256]{1,0:T(8,128)(2,1)} %w_key.1) | copy-start | bytes 393220
  71.5 63.6 %copy-start.9 = (bf16[256,256]{1,0:T(8,128)(2,1)S(1)}, bf16[256,256]{1,0:T(8,128)(2,1)}, u32[]{:S(2)}) copy-start(bf16[256,256]{1,0:T(8,128)(2,1)} %w_value.1) | copy-start | bytes 393220
  247.2 1.4 copy-start
  248.6 1.0 copy-start.1
  249.7 0.9 copy-start.2
  250.6 0.9 copy-start.3
  251.6 0.9 copy-start.4
  252.5 0.9 copy-start.5
  253.4 0.9 copy-start.6

commit v4 on v3

--- a/solution.py
+++ b/solution.py
@@ -1,5 +1,6 @@
 import jax
 import jax.numpy as jnp
+import numpy as np
 from jax import lax
 from jax.experimental import pallas as pl
 from jax.experimental.pallas import tpu as pltpu
@@ -951,7 +952,7 @@
         out_shape=[jax.ShapeDtypeStruct(*v) for v in shapes],
         in_specs=[spec] * 7,
         out_specs=[spec] * 11,
-        compiler_params=pltpu.CompilerParams(vmem_limit_bytes=40 * 1024 * 1024),
+        compiler_params=pltpu.CompilerParams(vmem_limit_bytes=63 * 1024 * 1024),
         name="finish",
     )(*operands)
 
@@ -972,11 +973,20 @@
     )(*operands)
 
 
-def rope_tables(positions):
+def rope_tables():
     half_dim = HEAD_DIM // 2
-    exponent = jnp.arange(half_dim).astype(F32) * (2.0 / HEAD_DIM)
-    angles = positions.astype(F32)[:, None] * (ROPE_BASE ** (-exponent))[None, :]
-    return (jnp.cos(angles), jnp.sin(angles))
+    exponent = np.arange(half_dim).astype(np.float32) * np.float32(2.0 / HEAD_DIM)
+    rates = np.power(np.float32(ROPE_BASE), -exponent).astype(np.float32)
+    angles = np.arange(LENGTH).astype(np.float32)[:, None] * rates[None, :]
+    cosine = np.cos(angles.astype(np.float64)).astype(np.float32)
+    sine_part = np.sin(angles.astype(np.float64)).astype(np.float32)
+    idle = np.zeros((LENGTH, HEAD_DIM), np.float32)
+    return (
+        np.concatenate([cosine] * 4, axis=1),
+        np.concatenate([sine_part, -sine_part] * 2, axis=1),
+        np.concatenate([cosine, cosine, idle + 1.0], axis=1),
+        np.concatenate([sine_part, -sine_part, idle], axis=1),
+    )
 
 
 def dot(a, b, dims):
@@ -999,14 +1009,7 @@
     w_up,
     w_down,
 ):
-    cosine, sine_part = rope_tables(jnp.arange(LENGTH, dtype=jnp.int32))
-    idle = jnp.zeros((LENGTH, HEAD_DIM), F32)
-    tables = (
-        jnp.concatenate([cosine] * 4, axis=1),
-        jnp.concatenate([sine_part, -sine_part] * 2, axis=1),
-        jnp.concatenate([cosine, cosine, idle + 1.0], axis=1),
-        jnp.concatenate([sine_part, -sine_part, idle], axis=1),
-    )
+    tables = [jnp.asarray(t, F32) for t in rope_tables()]
     router = w_router.T
     gain1, gain2 = norm_gain1.reshape(1, 256), norm_gain2.reshape(1, 256)
     (

time: 257 us -> 250 us (0.973)
  local copies, waits for them, and re-layouts: 7.84 us -> 1.36 us
    unnamed x20 -> x6, local copies, waits for them, and re-layouts: 7.12 us -> 0.02 us
where the time goes in v4:
time: 250 us
  Pallas kernels  247 us (99%)
    pallas_call x1, Pallas kernels, tail_step(): pl.pallas_call(tail_kernel, out_shape=[jax.ShapeDtypeStruct(*v) for v in...  112 us
    pallas_call x1, Pallas kernels, head_step(): pl.pallas_call(head_kernel, out_shape=[jax.ShapeDtypeStruct(*v) for v in...  68.3 us
    pallas_call x1, Pallas kernels, expert_step(): pl.pallas_call(expert_kernel, out_shape=[jax.ShapeDtypeStruct((LENGTH, 25...  63.7 us

profile of v4, /device:TPU:1, one launch (start us, length us, event | category | flops | bytes accessed | tf_op | source)
XLA Modules:
  0.0 250.2 jit_solution(12963613248719562937)
XLA Ops:
  0.6 68.3 %head.1 = (bf16[8,512,128]{2,1,0:T(8,128)(2,1)}, bf16[8,128,256]{2,1,0:T(8,128)(2,1)}, bf16[8,128,256]{2,1,0:T(8,128)(2,1)}, bf16[8,128,256]{2,1,0:T(8,128)(2,1)...) custom-call(bf16[512,256]{1,0:T(8,128)(2,1)} %x_in_ref.1, ...), custom_call_target="tpu_custom_call" | custom-call | tf_op jit(solution)/shard_map/head/pallas_call | solution.py:598
  68.9 0.0 copy-start
  69.0 0.0 copy-start.1
  69.0 0.0 copy-start.2
  69.0 63.7 %expert.1 = (bf16[512,256]{1,0:T(8,128)(2,1)}, f32[16,512]{1,0:T(8,128)}, bf16[16,80,256]{2,1,0:T(8,128)(2,1)}, bf16[16,80,256]{2,1,0:T(8,128)(2,1)}, bf16[8,3,128,256]{3,2,1,0:T(8,128)(2,1)}) custom-call(bf16[16,160,256]{2,1,0:T(8,128)(2,1)} %get-tuple-element.54.sent_x, bf16[16,160,256]{2,1,0:T(8,128)(2,1)} %get-tuple-element.55.sent_top, ...), custom_call_target="tpu_custom_call" | custom-call | tf_op jit(solution)/shard_map/expert/pallas_call | solution.py:300
  132.7 0.0 copy-done
  132.7 0.0 copy-done.1
  132.7 0.0 copy-done.2
  132.7 0.9 pad_maximum_fusion.whole_ref
  133.6 111.5 %tail.1 = (bf16[8,3,128,256]{3,2,1,0:T(8,128)(2,1)}, bf16[16,32,256]{2,1,0:T(8,128)(2,1)}, f32[16,8,256]{2,1,0:T(8,128)}, bf16[16,16,1024]{2,1,0:T(8,128)(2,1)},...) custom-call(bf16[512,256]{1,0:T(8,128)(2,1)} %get-tuple-element.61.home_ref, ...), custom_call_target="tpu_custom_call" | custom-call | tf_op jit(solution)/shard_map/tail/pallas_call | solution.py:962
  245.1 3.7 %finish.1 = (f32[2,256,256]{2,1,0:T(8,128)}, f32[2,256,256]{2,1,0:T(8,128)}, f32[2,256,256]{2,1,0:T(8,128)}, f32[256,512]{1,0:T(8,128)}, f32[256,256]{1,0:T(8,12...) custom-call(bf16[8,3,128,256]{3,2,1,0:T(8,128)(2,1)} %get-tuple-elem, ...), custom_call_target="tpu_custom_call" | custom-call | tf_op jit(solution)/shard_map/finish/pallas_call | solution.py:950
  248.8 1.3 fusion
Async XLA Ops:
  68.9 63.7 %copy-start = (bf16[256,512]{1,0:T(8,128)(2,1)S(1)}, bf16[256,512]{1,0:T(8,128)(2,1)}, u32[]{:S(2)}) copy-start(bf16[256,512]{1,0:T(8,128)(2,1)} %w_query.1) | copy-start | bytes 786436
  69.0 63.7 %copy-start.1 = (bf16[256,256]{1,0:T(8,128)(2,1)S(1)}, bf16[256,256]{1,0:T(8,128)(2,1)}, u32[]{:S(2)}) copy-start(bf16[256,256]{1,0:T(8,128)(2,1)} %w_key.1) | copy-start | bytes 393220
  69.0 63.7 %copy-start.2 = (bf16[256,256]{1,0:T(8,128)(2,1)S(1)}, bf16[256,256]{1,0:T(8,128)(2,1)}, u32[]{:S(2)}) copy-start(bf16[256,256]{1,0:T(8,128)(2,1)} %w_value.1) | copy-start | bytes 393220

commit v5 on v4

--- a/solution.py
+++ b/solution.py
@@ -174,8 +174,11 @@
         return 0
 
     lax.fori_loop(0, 4, forward, 0)
-    for copy in out_going[1] + out_going[2]:
+    for copy in out_going[1]:
         copy.wait()
+    early = [copy for copy, move in zip(out_going[2], steps) if move[1] == 2]
+    late = [copy for copy, move in zip(out_going[2], steps) if move[1] != 2]
+    late.append(out_going[2][-1])
 
     def home_of(s, j):
         place = {"dp": dp + 2 * (s - x), "row": j, "col": c}
@@ -197,6 +200,17 @@
 
     def backward(i, _):
         s = (x + 2 + i) % 4
+
+        @pl.when(i == 0)
+        def _():
+            for copy in early:
+                copy.wait()
+
+        @pl.when(i == 1)
+        def _():
+            for copy in late:
+                copy.wait()
+
         span = pl.ds(pl.multiple_of(s * CAP, CAP), CAP)
         top = jnp.concatenate([slots_top[4 * s + j] for j in range(4)], axis=1).astype(F32)
         p = jnp.transpose(slots_p[4 * s])[:CAP, :1]

time: 250 us -> 247 us (0.988)
  Pallas kernels: 247 us -> 244 us
    pallas_call x1, Pallas kernels: 112 us -> 108 us  [tail_step(): pl.pallas_call(tail_kernel, out_shape=[jax.ShapeDtypeStruct(*v) for v in...]
where the time goes in v5:
time: 247 us
  Pallas kernels  244 us (99%)
    pallas_call x1, Pallas kernels, tail_step(): pl.pallas_call(tail_kernel, out_shape=[jax.ShapeDtypeStruct(*v) for v in...  108 us
    pallas_call x1, Pallas kernels, head_step(): pl.pallas_call(head_kernel, out_shape=[jax.ShapeDtypeStruct(*v) for v in...  68.3 us
    pallas_call x1, Pallas kernels, expert_step(): pl.pallas_call(expert_kernel, out_shape=[jax.ShapeDtypeStruct((LENGTH, 25...  64.5 us

profile of v5, /device:TPU:1, one launch (start us, length us, event | category | flops | bytes accessed | tf_op | source)
XLA Modules:
  0.0 247.2 jit_solution(4817949530902376720)
XLA Ops:
  0.6 68.3 %head.1 = (bf16[8,512,128]{2,1,0:T(8,128)(2,1)}, bf16[8,128,256]{2,1,0:T(8,128)(2,1)}, bf16[8,128,256]{2,1,0:T(8,128)(2,1)}, bf16[8,128,256]{2,1,0:T(8,128)(2,1)...) custom-call(bf16[512,256]{1,0:T(8,128)(2,1)} %x_in_ref.1, ...), custom_call_target="tpu_custom_call" | custom-call | tf_op jit(solution)/shard_map/head/pallas_call | solution.py:612
  68.9 0.0 copy-start
  69.0 0.0 copy-start.1
  69.0 0.0 copy-start.2
  69.0 64.5 %expert.1 = (bf16[512,256]{1,0:T(8,128)(2,1)}, f32[16,512]{1,0:T(8,128)}, bf16[16,80,256]{2,1,0:T(8,128)(2,1)}, bf16[16,80,256]{2,1,0:T(8,128)(2,1)}, bf16[8,3,128,256]{3,2,1,0:T(8,128)(2,1)}) custom-call(bf16[16,160,256]{2,1,0:T(8,128)(2,1)} %get-tuple-element.54.sent_x, bf16[16,160,256]{2,1,0:T(8,128)(2,1)} %get-tuple-element.55.sent_top, ...), custom_call_target="tpu_custom_call" | custom-call | tf_op jit(solution)/shard_map/expert/pallas_call | solution.py:314
  133.5 0.0 copy-done
  133.5 0.0 copy-done.1
  133.6 0.0 copy-done.2
  133.6 0.9 pad_maximum_fusion.whole_ref
  134.4 107.7 %tail.1 = (bf16[8,3,128,256]{3,2,1,0:T(8,128)(2,1)}, bf16[16,32,256]{2,1,0:T(8,128)(2,1)}, f32[16,8,256]{2,1,0:T(8,128)}, bf16[16,16,1024]{2,1,0:T(8,128)(2,1)},...) custom-call(bf16[512,256]{1,0:T(8,128)(2,1)} %get-tuple-element.61.home_ref, ...), custom_call_target="tpu_custom_call" | custom-call | tf_op jit(solution)/shard_map/tail/pallas_call | solution.py:976
  242.1 3.7 %finish.1 = (f32[2,256,256]{2,1,0:T(8,128)}, f32[2,256,256]{2,1,0:T(8,128)}, f32[2,256,256]{2,1,0:T(8,128)}, f32[256,512]{1,0:T(8,128)}, f32[256,256]{1,0:T(8,12...) custom-call(bf16[8,3,128,256]{3,2,1,0:T(8,128)(2,1)} %get-tuple-elem, ...), custom_call_target="tpu_custom_call" | custom-call | tf_op jit(solution)/shard_map/finish/pallas_call | solution.py:964
  245.8 1.3 fusion
Async XLA Ops:
  68.9 64.6 %copy-start = (bf16[256,512]{1,0:T(8,128)(2,1)S(1)}, bf16[256,512]{1,0:T(8,128)(2,1)}, u32[]{:S(2)}) copy-start(bf16[256,512]{1,0:T(8,128)(2,1)} %w_query.1) | copy-start | bytes 786436
  69.0 64.6 %copy-start.1 = (bf16[256,256]{1,0:T(8,128)(2,1)S(1)}, bf16[256,256]{1,0:T(8,128)(2,1)}, u32[]{:S(2)}) copy-start(bf16[256,256]{1,0:T(8,128)(2,1)} %w_key.1) | copy-start | bytes 393220
  69.0 64.6 %copy-start.2 = (bf16[256,256]{1,0:T(8,128)(2,1)S(1)}, bf16[256,256]{1,0:T(8,128)(2,1)}, u32[]{:S(2)}) copy-start(bf16[256,256]{1,0:T(8,128)(2,1)} %w_value.1) | copy-start | bytes 393220
